TPU v7x, 256 devices: a whole 4x4x8 slice. The times are simulated.
256 devices in a mesh: grp: 2 (over core), dia: 32 (over y, z), rad: 4 (over x).
Axes of the slice: x: 4, y: 4, z: 8, core: 2. Of those that a mesh axis runs over, the one named last changes fastest.
Arguments:
- thermal_scalar: float32 [16, 2048, 128], P(None, ('grp', 'dia', 'rad')), may hold values from 0.5 to 8.5
- motion_vector_guess: float32 [3, 16, 2048, 128], P(None, 'rad', ('grp', 'dia')), may hold values from -4.5 to 4.5
- mean_stress_guess: float32 [16, 2048, 128], P('rad', ('grp', 'dia')), may hold values from -2 to 4
- flow_resistance_coefficient: float32 [16, 2048, 128], P('rad', ('grp', 'dia')), may hold values from 0.5 to 5
- flipped_junction_flags: int32 [16], replicated, may hold values 0 or 1
Outputs:
- velocity_out: float32 [3, 16, 2048, 128], P(None, 'rad', ('grp', 'dia'))
- pressure_out: float32 [16, 2048, 128], P('rad', ('grp', 'dia'))
- temperature_out: float32 [16, 2048, 128], P(None, ('grp', 'dia', 'rad'))
All inputs are finite; a program needn't handle non-finite values.
Results may differ from a plain program's by a relative error of at most 0.0003.
Values sent between devices are 32-bit elements; how exact they have to be, the bound alone decides.
A program may use at most 64 MiB of HBM per device.

v0:
```python
import functools

import jax
import jax.numpy as jnp
from jax import lax
from jax.experimental import pallas as pl
from jax.experimental.pallas import tpu as pltpu
from jax.sharding import PartitionSpec as P

DIA_ROWS = 128
OMEGA = 0.8
TAU = 0.25
RAYLEIGH = 4.0
KAPPA = 1.0
TIME_STEP = 0.1
MESH = pl.DeviceIdType.MESH

R0 = 8
HU = 5
HE = 4
IN = pl.ds(8, 16)
UP = pl.ds(9, 16)
DN = pl.ds(7, 16)
CIN = pl.ds(8, 8)
CUP = pl.ds(9, 8)
CDN = pl.ds(7, 8)
C0 = 9
A = 1.0 - OMEGA
B = OMEGA / 6.0


def rows(lo, hi, body, unroll=2):
    lax.fori_loop(lo, hi, lambda i, c: (body(i), c)[1], 0, unroll=unroll)


def column(ref, i):
    layers, width, lanes = ref.shape
    return ref.reshape(layers * width, lanes)[pl.ds(i, layers, stride=width)]


def set_column(ref, i, v):
    layers, width, lanes = ref.shape
    ref.reshape(layers * width, lanes)[pl.ds(i, layers, stride=width)] = v


def span(rt, halo):
    lo, hi = max(0, 8 * rt - halo), min(32, 8 * rt + 8 + halo)
    return lo, hi - lo, lo - 8 * rt + R0


def kernel(
    n_dia, n_chain, n_diamonds,
    t_ref, u_ref, p_ref, e_ref, flag_ref,
    uo_ref, po_ref, to_ref,
    rawu, rawp, rawe, rawt,
    U, PB, PF, EB, KB, TB, CB, DB, TMP,
    CS, CR, CU, CC, CE, CG, CP, X, HU_R, HP_R, OUT, TO,
    sgn, csgn, cflip,
    gs, gr, ls, hs, hr, xs, xr, os_, or_, ol,
):
    g = lax.axis_index("grp")
    d = lax.axis_index("dia")
    r = lax.axis_index("rad")
    k = g * n_dia + d
    c = k * 4 + r
    n_k = n_chain // 4

    def dev(ci):
        kk = lax.div(ci, 4)
        return (lax.div(kk, n_dia), lax.rem(kk, n_dia), lax.rem(ci, 4))

    def chain(step):
        return dev(lax.rem(c + step + n_chain, n_chain))

    barrier = pltpu.get_barrier_semaphore()
    for step in (1, -1, 2, -2, 3, -3, 4, -4):
        pl.semaphore_signal(barrier, inc=1, device_id=chain(step), device_id_type=MESH)

    layers = pl.ds(r * 4, 4)
    srcs = ((u_ref, rawu, HU, True), (p_ref, rawp, HU, False), (e_ref, rawe, HE, False))

    def cut(ref, vec, lay, start, size):
        sl = (lay, pl.ds(start, size), slice(None))
        return ref.at[(slice(None),) + sl] if vec else ref.at[sl]

    for rt in range(4):
        @pl.when(r == rt)
        def _():
            for n, (src, dst, halo, vec) in enumerate(srcs):
                lo, size, at = span(rt, halo)
                pltpu.make_async_copy(
                    cut(src, vec, slice(None), lo, size), cut(dst, vec, layers, at, size), ls.at[n]).start()
    pltpu.make_async_copy(t_ref, rawt.at[:, pl.ds(R0, 8)], ls.at[3]).start()

    per = DIA_ROWS // 32
    left = jnp.where((lax.rem(k, per) == 0) & (flag_ref[lax.div(k, per)] == 1), 1, 0)
    right = jnp.where(
        (lax.rem(k + 1, per) == 0) & (flag_ref[lax.rem(lax.div(k + 1, per), n_diamonds)] == 1), 1, 0)

    def flip_of(j, width, block):
        return jnp.where(j < -width * r, left, jnp.where(j >= block - width * r, right, 0))

    for i in range(24):
        sgn[i] = jnp.where(flip_of(i - R0, 8, 32) == 1, -1.0, 1.0)
    for i in range(22):
        csgn[i] = jnp.where(flip_of(i - C0, 4, 16) == 1, -1.0, 1.0)
    for n, J in enumerate((-4, -8, -12, 4, 8, 12)):
        cflip[n] = flip_of(J, 4, 16)
    flip_l, flip_r = flip_of(-1, 8, 32), flip_of(8, 8, 32)

    lane = lax.broadcasted_iota(jnp.int32, (16, 128), 1)
    clane = lax.broadcasted_iota(jnp.int32, (8, 128), 1)
    even = lax.rem(clane, 2) == 0
    back = 127 - lane
    cback = 127 - clane

    def lo1(v):
        return jnp.where(lane == 0, 0.0, pltpu.roll(v, 1, 1))

    def hi1(v):
        return jnp.where(lane == 127, 0.0, pltpu.roll(v, 127, 1))

    def lo2(v):
        return jnp.where(clane < 2, 0.0, pltpu.roll(v, 2, 1))

    def hi2(v):
        return jnp.where(clane >= 126, 0.0, pltpu.roll(v, 126, 1))

    z = jnp.zeros((8, 128), jnp.float32)

    def clear(i):
        for s in range(2):
            for q in range(3):
                U[s, q, i, pl.ds(0, 8)] = z
                U[s, q, i, pl.ds(24, 8)] = z
        for ref in (PB, PF, TB):
            ref[i, pl.ds(0, 8)] = z
            ref[i, pl.ds(24, 8)] = z

    rows(0, 24, clear, 1)

    def cclear(i):
        for s in range(2):
            for q in range(3):
                CU[s, q, i, pl.ds(0, 8)] = z
                CU[s, q, i, pl.ds(16, 8)] = z
        CP[i, pl.ds(0, 8)] = z
        CP[i, pl.ds(16, 8)] = z

    rows(0, 22, cclear, 1)

    pl.semaphore_wait(barrier, 8)

    def remote(src, dst, ssem, rsem, to):
        return pltpu.make_async_remote_copy(
            src_ref=src, dst_ref=dst, send_sem=ssem, recv_sem=rsem, device_id=to, device_id_type=MESH)

    for rt in (0, 1, 2, 3):
        @pl.when(r != rt)
        def _():
            for n, (src, dst, halo, vec) in enumerate(srcs):
                lo, size, at = span(rt, halo)
                remote(cut(src, vec, slice(None), lo, size), cut(dst, vec, layers, at, size),
                       gs.at[n, rt], gr.at[n], (g, d, rt)).start()
    nxt = lax.rem(k + 1, n_k)
    prv = lax.rem(k - 1 + n_k, n_k)
    to_next = (lax.div(nxt, n_dia), lax.rem(nxt, n_dia), 0)
    to_prev = (lax.div(prv, n_dia), lax.rem(prv, n_dia), 3)
    lateral = []
    for n, (src, dst, halo, vec) in enumerate(srcs):
        lateral.append(remote(cut(src, vec, slice(None), 32 - halo, halo), cut(dst, vec, layers, R0 - halo, halo),
                              gs.at[n, 4], gr.at[4 + n], to_next))
        lateral.append(remote(cut(src, vec, slice(None), 0, halo), cut(dst, vec, layers, R0 + 8, halo),
                              gs.at[n, 5], gr.at[4 + n], to_prev))
    lateral.append(remote(t_ref.at[:, pl.ds(8 - HE, HE)], rawt.at[:, pl.ds(R0 - HE, HE)],
                          gs.at[3, 0], gr.at[3], chain(1)))
    lateral.append(remote(t_ref.at[:, pl.ds(0, HE)], rawt.at[:, pl.ds(R0 + 8, HE)],
                          gs.at[3, 1], gr.at[3], chain(-1)))
    for copy in lateral:
        copy.start()

    def landed(ref, sem):
        pltpu.make_async_copy(ref, ref, sem).wait()

    for rt in range(4):
        @pl.when(r == rt)
        def _():
            for n, (src, dst, halo, vec) in enumerate(srcs):
                lo, size, at = span(rt, halo)
                own = cut(dst, vec, slice(0, 4), at, size)
                landed(own, ls.at[n])
                landed(cut(dst, vec, slice(0, 12), at, size), gr.at[n])
                if rt in (0, 3):
                    landed(cut(dst, vec, slice(0, 16), at, halo), gr.at[4 + n])
    landed(rawt.at[:, pl.ds(R0, 8)], ls.at[3])
    landed(rawt.at[:, pl.ds(R0, 2 * HE)], gr.at[3])

    def put(i, turn):
        for q in range(3):
            U[0, q, i, IN] = turn(column(rawu.at[q], i))
        PB[i, IN] = turn(column(rawp, i))
        EB[i] = turn(column(rawe, i))
        TB[i, IN] = turn(column(rawt, i))

    def turned(flag, idx):
        return lambda v: jnp.where(flag == 1, jnp.take_along_axis(v, idx, axis=1), v)

    rows(8, 16, lambda i: put(i, lambda v: v))
    rows(R0 - HU, R0, lambda i: put(i, turned(flip_l, back)), 1)
    rows(R0 + 8, R0 + 8 + HU, lambda i: put(i, turned(flip_r, back)), 1)

    def stencil(ref, s, q, i):
        v = ref[s, q, i, IN]
        total = (ref[s, q, i, UP] + ref[s, q, i, DN]) + (ref[s, q, i + 1, IN] + ref[s, q, i - 1, IN])
        return v, total + (lo1(v) + hi1(v))

    def sweep(s, i):
        for q in range(3):
            v, total = stencil(U, s, q, i)
            U[1 - s, q, i, IN] = A * v + B * total + CB[q, i]

    def slope(ref, i, sign):
        v = ref[i, IN]
        return (ref[i, UP] - ref[i, DN], ref[i + 1, IN] - ref[i - 1, IN], sign * (hi1(v) - lo1(v)))

    def diverge(s, i, sign):
        v = U[s, 2, i, IN]
        return 0.5 * ((U[s, 0, i, UP] - U[s, 0, i, DN]) + (U[s, 1, i + 1, IN] - U[s, 1, i - 1, IN])
                      + sign * (hi1(v) - lo1(v)))

    def push(press, kinv, i):
        gr_, ga_, gb_ = slope(press, i, sgn[i])
        half = -0.5 * kinv
        CB[0, i] = kinv * (RAYLEIGH * TB[i, IN]) + half * gr_
        CB[1, i] = half * ga_
        CB[2, i] = half * gb_

    def first(i):
        kinv = B / EB[i]
        KB[i] = kinv
        push(PB, kinv, i)
        sweep(0, i)

    rows(4, 20, first)
    rows(5, 19, lambda i: sweep(1, i))
    rows(6, 18, lambda i: sweep(0, i))

    def pre_pressure(i):
        div = diverge(1, i, sgn[i])
        DB[i] = div
        PB[i, IN] = PB[i, IN] - TAU * EB[i] * div

    rows(7, 17, pre_pressure)

    def coarse_row(m):
        i = R0 + 2 * m
        acc = [0.0] * 5
        for ii in (i, i + 1):
            gp = slope(PB, ii, 1.0)
            e = EB[ii]
            for q in range(3):
                v, total = stencil(U, 1, q, ii)
                res = -0.5 * gp[q] - e * (6.0 * v - total)
                if q == 0:
                    res = res + RAYLEIGH * TB[ii, IN]
                acc[q] = acc[q] + res
            acc[3] = acc[3] + e
            acc[4] = acc[4] + DB[ii]
        out = []
        for f in range(5):
            TMP[f, m] = acc[f]
        for f in range(5):
            v = TMP[f, m, pl.ds(0, 8, stride=2)] + TMP[f, m, pl.ds(1, 8, stride=2)]
            v = v + jnp.where(even, pltpu.roll(v, 127, 1), pltpu.roll(v, 1, 1))
            out.append(0.125 * v)
        kinv = (4.0 * B) / out[3]
        return [out[0] * kinv, out[1] * kinv, out[2] * kinv, out[3], out[4]]

    def coarse_put(I, vals):
        for q in range(3):
            CU[0, q, I, CIN] = vals[q]
            CC[q, I] = vals[q]
        CE[I] = vals[3]
        CG[I] = vals[4]

    def coarse_pair(h):
        first_row, second_row = coarse_row(2 * h), coarse_row(2 * h + 1)
        for f in range(5):
            CS[f, h] = jnp.where(even, first_row[f], second_row[f])
        coarse_put(C0 + 2 * h, first_row)
        coarse_put(C0 + 2 * h + 1, second_row)

    rows(0, 2, coarse_pair, 1)

    ex = [
        (remote(CS, CR.at[0], xs.at[0], xr.at[0], chain(1)), 1),
        (remote(CS, CR.at[3], xs.at[1], xr.at[3], chain(-1)), 1),
        (remote(CS.at[pl.ds(0, 3)], CR.at[1, pl.ds(0, 3)], xs.at[2], xr.at[1], chain(2)), 1),
        (remote(CS.at[pl.ds(0, 3)], CR.at[4, pl.ds(0, 3)], xs.at[3], xr.at[4], chain(-2)), 1),
        (remote(CS.at[pl.ds(0, 3), pl.ds(1, 1)], CR.at[2, pl.ds(0, 3), pl.ds(1, 1)], xs.at[4], xr.at[2], chain(3)), 1),
        (remote(CS.at[pl.ds(0, 3), pl.ds(0, 1)], CR.at[5, pl.ds(0, 3), pl.ds(0, 1)], xs.at[5], xr.at[5], chain(-3)), 1),
        (remote(CS.at[pl.ds(3, 2), pl.ds(1, 1)], CR.at[1, pl.ds(3, 2), pl.ds(1, 1)], xs.at[6], xr.at[6], chain(2)), 1),
        (remote(CS.at[pl.ds(3, 2), pl.ds(0, 1)], CR.at[4, pl.ds(3, 2), pl.ds(0, 1)], xs.at[7], xr.at[7], chain(-2)), 1),
    ]
    for copy, _ in ex:
        copy.start()
    halo = [
        remote(U.at[1, :, pl.ds(R0 + 4, 2), IN], HU_R.at[0], hs.at[0], hr.at[0], chain(1)),
        remote(U.at[1, :, pl.ds(R0 + 2, 2), IN], HU_R.at[1], hs.at[1], hr.at[1], chain(-1)),
        remote(PB.at[pl.ds(R0 + 4, 3), IN], HP_R.at[0], hs.at[2], hr.at[2], chain(1)),
        remote(PB.at[pl.ds(R0 + 1, 3), IN], HP_R.at[1], hs.at[3], hr.at[3], chain(-1)),
    ]
    for copy in halo:
        copy.start()
    for copy, _ in ex:
        copy.wait_recv()

    def unpack(x):
        return (jnp.where(even, x, pltpu.roll(x, 1, 1)), jnp.where(even, pltpu.roll(x, 127, 1), x))

    def take(n, f, h):
        turn = turned(cflip[n], cback)
        a, b = unpack(CR[n, f, h])
        return turn(a), turn(b)

    for n, base, fulls in ((0, -4, (0, 1)), (3, 4, (0, 1)), (1, -8, (1,)), (4, 8, (0,))):
        for h in (0, 1):
            I = C0 + base + 2 * h
            for q in range(3):
                a, b = take(n, q, h)
                for o, v in ((I, a), (I + 1, b)):
                    CU[0, q, o, CIN] = v
                    CC[q, o] = v
            if h in fulls:
                for f, ref in ((3, CE), (4, CG)):
                    a, b = take(n, f, h)
                    ref[I] = a
                    ref[I + 1] = b
    for q in range(3):
        CU[0, q, 0, CIN] = take(2, q, 1)[1]
        CU[0, q, 21, CIN] = take(5, q, 0)[0]

    def csweep(s, i):
        for q in range(3):
            v = CU[s, q, i, CIN]
            total = (CU[s, q, i, CUP] + CU[s, q, i, CDN]) + (CU[s, q, i + 1, CIN] + CU[s, q, i - 1, CIN])
            CU[1 - s, q, i, CIN] = A * v + B * (total + (lo2(v) + hi2(v))) + CC[q, i]

    def cdiverge(s, i):
        v = CU[s, 2, i, CIN]
        return 0.25 * ((CU[s, 0, i, CUP] - CU[s, 0, i, CDN]) + (CU[s, 1, i + 1, CIN] - CU[s, 1, i - 1, CIN])
                       + csgn[i] * (hi2(v) - lo2(v)))

    rows(1, 21, lambda i: csweep(0, i))
    rows(2, 20, lambda i: csweep(1, i))

    def cpress1(i):
        CP[i, CIN] = -TAU * CE[i] * (cdiverge(0, i) + CG[i])

    rows(3, 19, cpress1)

    def cfirst(i):
        v = CP[i, CIN]
        scale = (-B) / CE[i]
        CC[0, i] = CC[0, i] + scale * (CP[i, CUP] - CP[i, CDN])
        CC[1, i] = CC[1, i] + scale * (CP[i + 1, CIN] - CP[i - 1, CIN])
        CC[2, i] = CC[2, i] + scale * (csgn[i] * (hi2(v) - lo2(v)))
        csweep(0, i)

    rows(4, 18, cfirst)
    rows(5, 17, lambda i: csweep(1, i))
    rows(6, 16, lambda i: csweep(0, i))

    for copy in halo:
        copy.wait_recv()
    for side, flag, urow, prow in ((0, flip_l, 4, 4), (1, flip_r, 18, 17)):
        turn = turned(flag, back)
        for n in range(2):
            for q in range(3):
                U[1, q, urow + n, IN] = turn(HU_R[side, q, n])
        for n in range(3):
            PB[prow + n, IN] = turn(HP_R[side, n])

    def back_up(i):
        m = i - 7
        vals = [CU[1, 0, i, CIN], CU[1, 1, i, CIN], CU[1, 2, i, CIN],
                CP[i, CIN] - TAU * CE[i] * (cdiverge(1, i) + CG[i])]
        for f in range(4):
            X[f, m, pl.ds(0, 8, stride=2)] = vals[f]
            X[f, m, pl.ds(1, 8, stride=2)] = vals[f]
        for f in range(4):
            v = X[f, m]
            for n in range(2):
                row = 4 + 2 * m + n
                if f < 3:
                    U[0, f, row, IN] = U[1, f, row, IN] + v
                else:
                    PF[row, IN] = PB[row, IN] + v

    rows(7, 15, back_up)
    for copy in halo:
        copy.wait_send()

    def last_first(i):
        push(PF, KB[i], i)
        sweep(0, i)

    rows(5, 19, last_first)
    rows(6, 18, lambda i: sweep(1, i))
    rows(7, 17, lambda i: sweep(0, i))

    def finish(a):
        i = R0 + a
        for q in range(3):
            set_column(OUT.at[q], a, U[1, q, i, IN])
        set_column(OUT.at[3], a, PF[i, IN] - TAU * EB[i] * diverge(1, i, 1.0))
        t = TB[i, IN]
        up, dn, nx, pv, hi, lo = TB[i, UP], TB[i, DN], TB[i + 1, IN], TB[i - 1, IN], hi1(t), lo1(t)
        lap = 6.0 * t - (((up + dn) + (nx + pv)) + (hi + lo))
        carried = 0.5 * (U[1, 0, i, IN] * (up - dn) + U[1, 1, i, IN] * (nx - pv) + U[1, 2, i, IN] * (hi - lo))
        set_column(TO, a, t + TIME_STEP * (-KAPPA * lap - carried))

    rows(0, 8, finish)

    mine = pl.ds(pl.multiple_of(r * 8, 8), 8)
    for rt in range(4):
        lay = pl.ds(4 * rt, 4)

        @pl.when(r != rt)
        def _():
            remote(OUT.at[pl.ds(0, 3), lay], uo_ref.at[:, :, mine], os_.at[0, rt], or_.at[0], (g, d, rt)).start()
            remote(OUT.at[3, lay], po_ref.at[:, mine], os_.at[1, rt], or_.at[1], (g, d, rt)).start()

    own_u = pltpu.make_async_copy(OUT.at[pl.ds(0, 3), layers], uo_ref.at[:, :, mine], ol.at[0])
    own_p = pltpu.make_async_copy(OUT.at[3, layers], po_ref.at[:, mine], ol.at[1])
    own_t = pltpu.make_async_copy(TO, to_ref, ol.at[2])
    for copy in (own_u, own_p, own_t):
        copy.start()

    for copy in lateral:
        copy.wait_send()
    for copy, _ in ex:
        copy.wait_send()
    for rt in range(4):
        lay = pl.ds(4 * rt, 4)

        @pl.when(r != rt)
        def _():
            for n, (src, dst, halo_, vec) in enumerate(srcs):
                lo, size, at = span(rt, halo_)
                remote(cut(src, vec, slice(None), lo, size), cut(dst, vec, layers, at, size),
                       gs.at[n, rt], gr.at[n], (g, d, rt)).wait_send()
            remote(OUT.at[pl.ds(0, 3), lay], uo_ref.at[:, :, mine], os_.at[0, rt], or_.at[0], (g, d, rt)).wait_send()
            remote(OUT.at[3, lay], po_ref.at[:, mine], os_.at[1, rt], or_.at[1], (g, d, rt)).wait_send()
    for copy in (own_u, own_p, own_t):
        copy.wait()
    landed(uo_ref.at[:, :, pl.ds(0, 24)], or_.at[0])
    landed(po_ref.at[:, pl.ds(0, 24)], or_.at[1])


def per_device(n_dia, n_chain, t, u, p, e, flags):
    f32 = jnp.float32
    V = pltpu.VMEM
    DMA = pltpu.SemaphoreType.DMA
    any_ = pl.BlockSpec(memory_space=pl.ANY)
    return pl.pallas_call(
        functools.partial(kernel, n_dia, n_chain, flags.shape[0]),
        out_shape=(
            jax.ShapeDtypeStruct(u.shape, f32),
            jax.ShapeDtypeStruct(p.shape, f32),
            jax.ShapeDtypeStruct(t.shape, f32),
        ),
        in_specs=[any_] * 4 + [pl.BlockSpec(memory_space=pltpu.SMEM)],
        out_specs=(any_,) * 3,
        scratch_shapes=[
            V((3, 16, 24, 128), f32), V((16, 24, 128), f32), V((16, 24, 128), f32), V((16, 24, 128), f32),
            V((2, 3, 24, 32, 128), f32), V((24, 32, 128), f32), V((24, 32, 128), f32),
            V((24, 16, 128), f32), V((24, 16, 128), f32), V((24, 32, 128), f32),
            V((3, 24, 16, 128), f32), V((24, 16, 128), f32), V((5, 4, 16, 128), f32),
            V((5, 2, 8, 128), f32), V((6, 5, 2, 8, 128), f32),
            V((2, 3, 22, 24, 128), f32), V((3, 22, 8, 128), f32), V((22, 8, 128), f32), V((22, 8, 128), f32),
            V((22, 24, 128), f32), V((4, 8, 16, 128), f32),
            V((2, 3, 2, 16, 128), f32), V((2, 3, 16, 128), f32),
            V((4, 16, 8, 128), f32), V((16, 8, 128), f32),
            pltpu.SMEM((24,), f32), pltpu.SMEM((22,), f32), pltpu.SMEM((6,), jnp.int32),
            DMA((4, 6)), DMA((7,)), DMA((4,)), DMA((4,)), DMA((4,)), DMA((8,)), DMA((8,)),
            DMA((2, 4)), DMA((2,)), DMA((3,)),
        ],
        compiler_params=pltpu.CompilerParams(collective_id=0, has_side_effects=True),
        name="cycle",
    )(t, u, p, e, flags)


def solution(mesh):
    n_dia = mesh.shape["dia"]
    n_chain = n_dia * mesh.shape["grp"] * mesh.shape["rad"]
    return jax.shard_map(
        functools.partial(per_device, n_dia, n_chain),
        mesh=mesh,
        in_specs=(
            P(None, ("grp", "dia", "rad"), None),
            P(None, "rad", ("grp", "dia"), None),
            P("rad", ("grp", "dia"), None),
            P("rad", ("grp", "dia"), None),
            P(),
        ),
        out_specs=(
            P(None, "rad", ("grp", "dia"), None),
            P("rad", ("grp", "dia"), None),
            P(None, ("grp", "dia", "rad"), None),
        ),
        check_vma=False,
    )
```

profile of v0, /device:TPU:1, one launch (start us, length us, event | category | flops | bytes accessed | tf_op | source)
XLA Modules:
  0.0 49.6 jit_solution(14444569116156613181)
XLA Ops:
  0.6 45.8 %cycle.1 = (f32[3,4,32,128]{3,2,1,0:T(8,128)}, f32[4,32,128]{2,1,0:T(8,128)}, f32[16,8,128]{2,1,0:T(8,128)}) custom-call(f32[16,8,128]{2,1,0:T(8,128)} %t_ref.1, f32[3,4,32,128]{3,2,1,0:T(8,128)} %u_ref.1, f32[4,32,128]{2,1,0:T(8,128)} %p_ref.1, f32[4,32,128]{2,1,0:T(8,128)} %e_ref.1, s32[16]{0:T(128)} %flag_ref.1), custom_call_target="tpu_custom_call" | custom-call | tf_op jit(solution)/shard_map/cycle/pallas_call | solution.py:466
  46.4 0.0 copy-start.1
  46.4 1.6 %copy.11 = f32[3,4,32,128]{3,2,1,0:T(8,128)} copy(f32[3,4,32,128]{3,2,1,0:T(8,128)} %get-tuple-element.6) | data formatting | bytes 393216
  48.1 0.0 copy-done.1
  48.1 0.0 copy-start
  48.1 0.6 %copy.12 = f32[4,32,128]{2,1,0:T(8,128)} copy(f32[4,32,128]{2,1,0:T(8,128)S(1)} %copy-done.1) | data formatting | bytes 131072
  48.7 0.2 copy-done
  48.9 0.6 %copy.13 = f32[16,8,128]{2,1,0:T(8,128)} copy(f32[16,8,128]{2,1,0:T(8,128)S(1)} %copy-done) | data formatting | bytes 131072
Async XLA Ops:
  46.4 1.7 %copy-start.1 = (f32[4,32,128]{2,1,0:T(8,128)S(1)}, f32[4,32,128]{2,1,0:T(8,128)}, u32[]{:S(2)}) copy-start(f32[4,32,128]{2,1,0:T(8,128)} %get-tuple-element.7) | copy-start | bytes 196612
  48.1 0.9 %copy-start = (f32[16,8,128]{2,1,0:T(8,128)S(1)}, f32[16,8,128]{2,1,0:T(8,128)}, u32[]{:S(2)}) copy-start(f32[16,8,128]{2,1,0:T(8,128)} %get-tuple-element.8) | copy-start | bytes 196612
where the time goes:
time: 49.7 us; the launch traced here: 49.6 us
  Pallas kernels  45.8 us (92%)
  local copies, waits for them, and re-layouts  3.14 us (6%)
  between operations  0.65 us (1%)
    pallas_call x1, Pallas kernels, per_device(): pl.pallas_call(functools.partial(kernel, n_dia, n_chain, flags.shape[0]),...  45.8 us
    unnamed x7, local copies, waits for them, and re-layouts  3.14 us

commit v1 on v0

--- a/solution.py
+++ b/solution.py
@@ -29,7 +29,8 @@
 B = OMEGA / 6.0
 
 
-def rows(lo, hi, body, unroll=2):
+def rows(lo, hi, body, unroll=None):
+    unroll = hi - lo if unroll is None else unroll
     lax.fori_loop(lo, hi, lambda i, c: (body(i), c)[1], 0, unroll=unroll)
 
 
@@ -54,7 +55,7 @@
     uo_ref, po_ref, to_ref,
     rawu, rawp, rawe, rawt,
     U, PB, PF, EB, KB, TB, CB, DB, TMP,
-    CS, CR, CU, CC, CE, CG, CP, X, HU_R, HP_R, OUT, TO,
+    CS, CR, CU, CC, CE, CG, CP, X, HU_R, HP_R, OUT,
     sgn, csgn, cflip,
     gs, gr, ls, hs, hr, xs, xr, os_, or_, ol,
 ):
@@ -77,7 +78,7 @@
         pl.semaphore_signal(barrier, inc=1, device_id=chain(step), device_id_type=MESH)
 
     layers = pl.ds(r * 4, 4)
-    srcs = ((u_ref, rawu, HU, True), (p_ref, rawp, HU, False), (e_ref, rawe, HE, False))
+    srcs = ((p_ref, rawp, HU, False), (e_ref, rawe, HE, False), (u_ref, rawu, HU, True))
 
     def cut(ref, vec, lay, start, size):
         sl = (lay, pl.ds(start, size), slice(None))
@@ -155,59 +156,68 @@
         return pltpu.make_async_remote_copy(
             src_ref=src, dst_ref=dst, send_sem=ssem, recv_sem=rsem, device_id=to, device_id_type=MESH)
 
-    for rt in (0, 1, 2, 3):
-        @pl.when(r != rt)
-        def _():
-            for n, (src, dst, halo, vec) in enumerate(srcs):
-                lo, size, at = span(rt, halo)
-                remote(cut(src, vec, slice(None), lo, size), cut(dst, vec, layers, at, size),
-                       gs.at[n, rt], gr.at[n], (g, d, rt)).start()
     nxt = lax.rem(k + 1, n_k)
     prv = lax.rem(k - 1 + n_k, n_k)
     to_next = (lax.div(nxt, n_dia), lax.rem(nxt, n_dia), 0)
     to_prev = (lax.div(prv, n_dia), lax.rem(prv, n_dia), 3)
     lateral = []
     for n, (src, dst, halo, vec) in enumerate(srcs):
-        lateral.append(remote(cut(src, vec, slice(None), 32 - halo, halo), cut(dst, vec, layers, R0 - halo, halo),
-                              gs.at[n, 4], gr.at[4 + n], to_next))
-        lateral.append(remote(cut(src, vec, slice(None), 0, halo), cut(dst, vec, layers, R0 + 8, halo),
-                              gs.at[n, 5], gr.at[4 + n], to_prev))
-    lateral.append(remote(t_ref.at[:, pl.ds(8 - HE, HE)], rawt.at[:, pl.ds(R0 - HE, HE)],
-                          gs.at[3, 0], gr.at[3], chain(1)))
-    lateral.append(remote(t_ref.at[:, pl.ds(0, HE)], rawt.at[:, pl.ds(R0 + 8, HE)],
-                          gs.at[3, 1], gr.at[3], chain(-1)))
-    for copy in lateral:
-        copy.start()
+        here = [
+            remote(cut(src, vec, slice(None), 32 - halo, halo), cut(dst, vec, layers, R0 - halo, halo),
+                   gs.at[n, 4], gr.at[4 + n], to_next),
+            remote(cut(src, vec, slice(None), 0, halo), cut(dst, vec, layers, R0 + 8, halo),
+                   gs.at[n, 5], gr.at[4 + n], to_prev)]
+        if n == 0:
+            here += [
+                remote(t_ref.at[:, pl.ds(8 - HE, HE)], rawt.at[:, pl.ds(R0 - HE, HE)], gs.at[3, 0], gr.at[3], chain(1)),
+                remote(t_ref.at[:, pl.ds(0, HE)], rawt.at[:, pl.ds(R0 + 8, HE)], gs.at[3, 1], gr.at[3], chain(-1))]
+        for copy in here:
+            copy.start()
+        lateral += here
+        for rt in (0, 1, 2, 3):
+            @pl.when(r != rt)
+            def _():
+                lo, size, at = span(rt, halo)
+                remote(cut(src, vec, slice(None), lo, size), cut(dst, vec, layers, at, size),
+                       gs.at[n, rt], gr.at[n], (g, d, rt)).start()
 
     def landed(ref, sem):
         pltpu.make_async_copy(ref, ref, sem).wait()
 
-    for rt in range(4):
-        @pl.when(r == rt)
-        def _():
-            for n, (src, dst, halo, vec) in enumerate(srcs):
-                lo, size, at = span(rt, halo)
-                own = cut(dst, vec, slice(0, 4), at, size)
-                landed(own, ls.at[n])
-                landed(cut(dst, vec, slice(0, 12), at, size), gr.at[n])
-                if rt in (0, 3):
-                    landed(cut(dst, vec, slice(0, 16), at, halo), gr.at[4 + n])
+    def gathered(which):
+        for rt in range(4):
+            @pl.when(r == rt)
+            def _():
+                for n in which:
+                    src, dst, halo, vec = srcs[n]
+                    lo, size, at = span(rt, halo)
+                    landed(cut(dst, vec, slice(0, 4), at, size), ls.at[n])
+                    landed(cut(dst, vec, slice(0, 12), at, size), gr.at[n])
+                    if rt in (0, 3):
+                        landed(cut(dst, vec, slice(0, 16), at, halo), gr.at[4 + n])
+
+    gathered((0, 1))
     landed(rawt.at[:, pl.ds(R0, 8)], ls.at[3])
     landed(rawt.at[:, pl.ds(R0, 2 * HE)], gr.at[3])
 
-    def put(i, turn):
-        for q in range(3):
-            U[0, q, i, IN] = turn(column(rawu.at[q], i))
+    def put_scalars(i, turn):
         PB[i, IN] = turn(column(rawp, i))
         EB[i] = turn(column(rawe, i))
         TB[i, IN] = turn(column(rawt, i))
 
+    def put_vector(i, turn):
+        for q in range(3):
+            U[0, q, i, IN] = turn(column(rawu.at[q], i))
+
     def turned(flag, idx):
         return lambda v: jnp.where(flag == 1, jnp.take_along_axis(v, idx, axis=1), v)
 
-    rows(8, 16, lambda i: put(i, lambda v: v))
-    rows(R0 - HU, R0, lambda i: put(i, turned(flip_l, back)), 1)
-    rows(R0 + 8, R0 + 8 + HU, lambda i: put(i, turned(flip_r, back)), 1)
+    def put_all(put):
+        rows(8, 16, lambda i: put(i, lambda v: v))
+        rows(R0 - HU, R0, lambda i: put(i, turned(flip_l, back)))
+        rows(R0 + 8, R0 + 8 + HU, lambda i: put(i, turned(flip_r, back)))
+
+    put_all(put_scalars)
 
     def stencil(ref, s, q, i):
         v = ref[s, q, i, IN]
@@ -235,13 +245,15 @@
         CB[1, i] = half * ga_
         CB[2, i] = half * gb_
 
-    def first(i):
+    def first_push(i):
         kinv = B / EB[i]
         KB[i] = kinv
         push(PB, kinv, i)
-        sweep(0, i)
-
-    rows(4, 20, first)
+
+    rows(4, 20, first_push)
+    gathered((2,))
+    put_all(put_vector)
+    rows(4, 20, lambda i: sweep(0, i))
     rows(5, 19, lambda i: sweep(1, i))
     rows(6, 18, lambda i: sweep(0, i))
 
@@ -290,7 +302,7 @@
         coarse_put(C0 + 2 * h, first_row)
         coarse_put(C0 + 2 * h + 1, second_row)
 
-    rows(0, 2, coarse_pair, 1)
+    rows(0, 2, coarse_pair)
 
     ex = [
         (remote(CS, CR.at[0], xs.at[0], xr.at[0], chain(1)), 1),
@@ -409,53 +421,67 @@
     rows(6, 18, lambda i: sweep(1, i))
     rows(7, 17, lambda i: sweep(0, i))
 
-    def finish(a):
+    def finish_u(a):
+        for q in range(3):
+            set_column(OUT.at[q], a, U[1, q, R0 + a, IN])
+
+    def finish_p(a):
         i = R0 + a
-        for q in range(3):
-            set_column(OUT.at[q], a, U[1, q, i, IN])
         set_column(OUT.at[3], a, PF[i, IN] - TAU * EB[i] * diverge(1, i, 1.0))
+
+    def finish_t(a):
+        i = R0 + a
         t = TB[i, IN]
         up, dn, nx, pv, hi, lo = TB[i, UP], TB[i, DN], TB[i + 1, IN], TB[i - 1, IN], hi1(t), lo1(t)
         lap = 6.0 * t - (((up + dn) + (nx + pv)) + (hi + lo))
         carried = 0.5 * (U[1, 0, i, IN] * (up - dn) + U[1, 1, i, IN] * (nx - pv) + U[1, 2, i, IN] * (hi - lo))
-        set_column(TO, a, t + TIME_STEP * (-KAPPA * lap - carried))
-
-    rows(0, 8, finish)
+        set_column(to_ref, a, t + TIME_STEP * (-KAPPA * lap - carried))
 
     mine = pl.ds(pl.multiple_of(r * 8, 8), 8)
-    for rt in range(4):
-        lay = pl.ds(4 * rt, 4)
-
-        @pl.when(r != rt)
-        def _():
-            remote(OUT.at[pl.ds(0, 3), lay], uo_ref.at[:, :, mine], os_.at[0, rt], or_.at[0], (g, d, rt)).start()
-            remote(OUT.at[3, lay], po_ref.at[:, mine], os_.at[1, rt], or_.at[1], (g, d, rt)).start()
-
     own_u = pltpu.make_async_copy(OUT.at[pl.ds(0, 3), layers], uo_ref.at[:, :, mine], ol.at[0])
     own_p = pltpu.make_async_copy(OUT.at[3, layers], po_ref.at[:, mine], ol.at[1])
-    own_t = pltpu.make_async_copy(TO, to_ref, ol.at[2])
-    for copy in (own_u, own_p, own_t):
-        copy.start()
+
+    def home_u(rt):
+        return remote(OUT.at[pl.ds(0, 3), pl.ds(4 * rt, 4)], uo_ref.at[:, :, mine], os_.at[0, rt], or_.at[0], (g, d, rt))
+
+    def home_p(rt):
+        return remote(OUT.at[3, pl.ds(4 * rt, 4)], po_ref.at[:, mine], os_.at[1, rt], or_.at[1], (g, d, rt))
+
+    for finish, home, own in ((finish_u, home_u, own_u), (finish_p, home_p, own_p)):
+        rows(0, 8, finish)
+        for rt in range(4):
+            @pl.when(r != rt)
+            def _():
+                home(rt).start()
+        own.start()
+    rows(0, 8, finish_t)
 
     for copy in lateral:
         copy.wait_send()
     for copy, _ in ex:
         copy.wait_send()
     for rt in range(4):
-        lay = pl.ds(4 * rt, 4)
-
         @pl.when(r != rt)
         def _():
             for n, (src, dst, halo_, vec) in enumerate(srcs):
                 lo, size, at = span(rt, halo_)
                 remote(cut(src, vec, slice(None), lo, size), cut(dst, vec, layers, at, size),
                        gs.at[n, rt], gr.at[n], (g, d, rt)).wait_send()
-            remote(OUT.at[pl.ds(0, 3), lay], uo_ref.at[:, :, mine], os_.at[0, rt], or_.at[0], (g, d, rt)).wait_send()
-            remote(OUT.at[3, lay], po_ref.at[:, mine], os_.at[1, rt], or_.at[1], (g, d, rt)).wait_send()
-    for copy in (own_u, own_p, own_t):
+            home_u(rt).wait_send()
+            home_p(rt).wait_send()
+    for copy in (own_u, own_p):
         copy.wait()
     landed(uo_ref.at[:, :, pl.ds(0, 24)], or_.at[0])
     landed(po_ref.at[:, pl.ds(0, 24)], or_.at[1])
+
+
+def write_out(*refs):
+    sem = refs[6]
+    copies = [pltpu.make_async_copy(refs[n], refs[3 + n], sem.at[n]) for n in range(3)]
+    for copy in copies:
+        copy.start()
+    for copy in copies:
+        copy.wait()
 
 
 def per_device(n_dia, n_chain, t, u, p, e, flags):
@@ -463,15 +489,16 @@
     V = pltpu.VMEM
     DMA = pltpu.SemaphoreType.DMA
     any_ = pl.BlockSpec(memory_space=pl.ANY)
-    return pl.pallas_call(
+    vmem = pl.BlockSpec(memory_space=pltpu.VMEM)
+    done = pl.pallas_call(
         functools.partial(kernel, n_dia, n_chain, flags.shape[0]),
         out_shape=(
-            jax.ShapeDtypeStruct(u.shape, f32),
-            jax.ShapeDtypeStruct(p.shape, f32),
-            jax.ShapeDtypeStruct(t.shape, f32),
+            V(u.shape, f32),
+            V(p.shape, f32),
+            V(t.shape, f32),
         ),
         in_specs=[any_] * 4 + [pl.BlockSpec(memory_space=pltpu.SMEM)],
-        out_specs=(any_,) * 3,
+        out_specs=(vmem,) * 3,
         scratch_shapes=[
             V((3, 16, 24, 128), f32), V((16, 24, 128), f32), V((16, 24, 128), f32), V((16, 24, 128), f32),
             V((2, 3, 24, 32, 128), f32), V((24, 32, 128), f32), V((24, 32, 128), f32),
@@ -481,14 +508,22 @@
             V((2, 3, 22, 24, 128), f32), V((3, 22, 8, 128), f32), V((22, 8, 128), f32), V((22, 8, 128), f32),
             V((22, 24, 128), f32), V((4, 8, 16, 128), f32),
             V((2, 3, 2, 16, 128), f32), V((2, 3, 16, 128), f32),
-            V((4, 16, 8, 128), f32), V((16, 8, 128), f32),
+            V((4, 16, 8, 128), f32),
             pltpu.SMEM((24,), f32), pltpu.SMEM((22,), f32), pltpu.SMEM((6,), jnp.int32),
             DMA((4, 6)), DMA((7,)), DMA((4,)), DMA((4,)), DMA((4,)), DMA((8,)), DMA((8,)),
-            DMA((2, 4)), DMA((2,)), DMA((3,)),
+            DMA((2, 4)), DMA((2,)), DMA((2,)),
         ],
         compiler_params=pltpu.CompilerParams(collective_id=0, has_side_effects=True),
         name="cycle",
     )(t, u, p, e, flags)
+    return pl.pallas_call(
+        write_out,
+        out_shape=[jax.ShapeDtypeStruct(x.shape, f32) for x in done],
+        in_specs=[vmem] * 3,
+        out_specs=[any_] * 3,
+        scratch_shapes=[DMA((3,))],
+        name="write_out",
+    )(*[pltpu.with_memory_space_constraint(x, pltpu.VMEM) for x in done])
 
 
 def solution(mesh):

time: 49.7 us -> 39 us (0.78)
  Pallas kernels: 45.8 us -> 38.3 us
  local copies, waits for them, and re-layouts: 3.14 us -> 0 us
    pallas_call x1, Pallas kernels: 45.8 us -> 37.5 us  [per_device(): pl.pallas_call(functools.partial(kernel, n_dia, n_chain, flags.shape[0]),...]
    unnamed x7 -> x0, local copies, waits for them, and re-layouts: 3.14 us -> none
    pallas_call x0 -> x1, Pallas kernels: none -> 0.74 us  [per_device(): pl.pallas_call(write_out, out_shape=[jax.ShapeDtypeStruct(x.shape, f32) f...]
where the time goes in v1:
time: 39 us; the launch traced here: 38.9 us
  Pallas kernels  38.3 us (98%)
  between operations  0.64 us (2%)
    pallas_call x1, Pallas kernels, per_device(): pl.pallas_call(functools.partial(kernel, n_dia, n_chain, flags.shape[0]),...  37.5 us

profile of v1, /device:TPU:1, one launch (start us, length us, event | category | flops | bytes accessed | tf_op | source)
XLA Modules:
  0.0 38.9 jit_solution(9876160258654778947)
XLA Ops:
  0.6 37.5 %cycle.1 = (f32[3,4,32,128]{3,2,1,0:T(8,128)S(1)}, f32[4,32,128]{2,1,0:T(8,128)S(1)}, f32[16,8,128]{2,1,0:T(8,128)S(1)}) custom-call(f32[16,8,128]{2,1,0:T(8,128)} %t_ref.1, f32[3,4,32,128]{3,2,1,0:T(8,128)} %u_ref.1, f32[4,32,128]{2,1,0:T(8,128)} %p_ref.1, f32[4,32,128]{2,1,0:T(8,128)} %e_ref.1, s32[16]{0:T(128)} %flag_ref.1), custom_call_target="tpu_custom_call" | custom-call | tf_op jit(solution)/shard_map/cycle/pallas_call | solution.py:493
  38.2 0.7 %write_out.1 = (f32[3,4,32,128]{3,2,1,0:T(8,128)}, f32[4,32,128]{2,1,0:T(8,128)}, f32[16,8,128]{2,1,0:T(8,128)}) custom-call(f32[3,4,32,128]{3,2,1,0:T(8,128)S(1)} %get-tuple-element.6.refs_0_, f32[4,32,128]{2,1,0:T(8,128)S(1)} %get-tuple-element.7.refs_1_, f32[16,8,128]{2,1,0:T(8,128)S(1)} %get-tuple-element.8.refs_2_), custom_call_target="tpu_custom_call" | custom-call | tf_op jit(solution)/shard_map/write_out/pallas_call | solution.py:519

commit v2 on v1

v2 whole, which is shorter than its diff:
```python
import functools

import jax
import jax.numpy as jnp
from jax import lax
from jax.experimental import pallas as pl
from jax.experimental.pallas import tpu as pltpu
from jax.sharding import PartitionSpec as P

DIA_ROWS = 128
OMEGA = 0.8
TAU = 0.25
RAYLEIGH = 4.0
KAPPA = 1.0
TIME_STEP = 0.1
MESH = pl.DeviceIdType.MESH

R0 = 8
HU = 5
HE = 4
IN = pl.ds(8, 16)
UP = pl.ds(9, 16)
DN = pl.ds(7, 16)
CIN = pl.ds(8, 8)
CUP = pl.ds(9, 8)
CDN = pl.ds(7, 8)
C0 = 9
A = 1.0 - OMEGA
B = OMEGA / 6.0


def rows(lo, hi, body, unroll=None):
    unroll = hi - lo if unroll is None else unroll
    lax.fori_loop(lo, hi, lambda i, c: (body(i), c)[1], 0, unroll=unroll)


def column(ref, i):
    layers, width, lanes = ref.shape
    return ref.reshape(layers * width, lanes)[pl.ds(i, layers, stride=width)]


def set_column(ref, i, v):
    layers, width, lanes = ref.shape
    ref.reshape(layers * width, lanes)[pl.ds(i, layers, stride=width)] = v


def span(rt, halo):
    lo, hi = max(0, 8 * rt - halo), min(32, 8 * rt + 8 + halo)
    return lo, hi - lo, lo - 8 * rt + R0


def kernel(
    n_dia, n_chain, n_diamonds,
    t_ref, u_ref, p_ref, e_ref, flag_hbm,
    uo_ref, po_ref, to_ref,
    rawu, rawp, rawe, rawt,
    U, PB, PF, EB, KB, TB, CB, DB, TMP,
    CS, CR, CU, CC, CE, CG, CP, X, HU_R, HP_R, OUT,
    flag_ref, sgn, csgn, cflip,
    gs, gr, ls, hs, hr, xs, xr, os_, or_, ol, fs,
):
    g = lax.axis_index("grp")
    d = lax.axis_index("dia")
    r = lax.axis_index("rad")
    k = g * n_dia + d
    c = k * 4 + r
    n_k = n_chain // 4

    def dev(ci):
        kk = lax.div(ci, 4)
        return (lax.div(kk, n_dia), lax.rem(kk, n_dia), lax.rem(ci, 4))

    def chain(step):
        return dev(lax.rem(c + step + n_chain, n_chain))

    barrier = pltpu.get_barrier_semaphore()
    for step in (1, -1, 2, -2, 3, -3, 4, -4):
        pl.semaphore_signal(barrier, inc=1, device_id=chain(step), device_id_type=MESH)

    pl.semaphore_wait(barrier, 8)

    layers = pl.ds(r * 4, 4)
    srcs = ((p_ref, rawp, HU), (e_ref, rawe, HE)) + tuple((u_ref.at[q], rawu.at[q], HU) for q in range(3))

    def cut(ref, lay, start, size):
        return ref.at[lay, pl.ds(start, size)]

    def remote(src, dst, ssem, rsem, to):
        return pltpu.make_async_remote_copy(
            src_ref=src, dst_ref=dst, send_sem=ssem, recv_sem=rsem, device_id=to, device_id_type=MESH)

    nxt = lax.rem(k + 1, n_k)
    prv = lax.rem(k - 1 + n_k, n_k)
    to_next = (lax.div(nxt, n_dia), lax.rem(nxt, n_dia), 0)
    to_prev = (lax.div(prv, n_dia), lax.rem(prv, n_dia), 3)

    def lateral(n):
        src, dst, halo = srcs[n]
        return [
            remote(cut(src, slice(None), 32 - halo, halo), cut(dst, layers, R0 - halo, halo),
                   gs.at[n, 4], gr.at[5 + n], to_next),
            remote(cut(src, slice(None), 0, halo), cut(dst, layers, R0 + 8, halo),
                   gs.at[n, 5], gr.at[5 + n], to_prev)]

    def across(n, rt):
        src, dst, halo = srcs[n]
        lo, size, at = span(rt, halo)
        return remote(cut(src, slice(None), lo, size), cut(dst, layers, at, size), gs.at[n, rt], gr.at[n], (g, d, rt))

    heat = [
        remote(t_ref.at[:, pl.ds(8 - HE, HE)], rawt.at[:, pl.ds(R0 - HE, HE)], gs.at[5, 0], gr.at[10], chain(1)),
        remote(t_ref.at[:, pl.ds(0, HE)], rawt.at[:, pl.ds(R0 + 8, HE)], gs.at[5, 1], gr.at[10], chain(-1))]
    for rs in range(4):
        @pl.when(r == rs)
        def _():
            for n in range(5):
                for copy in lateral(n):
                    copy.start()
                for step in (2, 1, 3):
                    across(n, (rs + step) % 4).start()
                if n == 1:
                    for copy in heat:
                        copy.start()

    read_flags = pltpu.make_async_copy(flag_hbm, flag_ref, fs)
    read_flags.start()
    for rt in range(4):
        @pl.when(r == rt)
        def _():
            for n, (src, dst, halo) in enumerate(srcs):
                lo, size, at = span(rt, halo)
                pltpu.make_async_copy(cut(src, slice(None), lo, size), cut(dst, layers, at, size), ls.at[n]).start()
    pltpu.make_async_copy(t_ref, rawt.at[:, pl.ds(R0, 8)], ls.at[5]).start()

    z = jnp.zeros((8, 128), jnp.float32)

    def clear(i):
        for s in range(2):
            for q in range(3):
                U[s, q, i, pl.ds(0, 8)] = z
                U[s, q, i, pl.ds(24, 8)] = z
        for ref in (PB, PF, TB):
            ref[i, pl.ds(0, 8)] = z
            ref[i, pl.ds(24, 8)] = z

    rows(0, 24, clear, 1)

    def cclear(i):
        for s in range(2):
            for q in range(3):
                CU[s, q, i, pl.ds(0, 8)] = z
                CU[s, q, i, pl.ds(16, 8)] = z
        CP[i, pl.ds(0, 8)] = z
        CP[i, pl.ds(16, 8)] = z

    rows(0, 22, cclear, 1)

    read_flags.wait()
    per = DIA_ROWS // 32
    left = jnp.where((lax.rem(k, per) == 0) & (flag_ref[lax.div(k, per)] == 1), 1, 0)
    right = jnp.where(
        (lax.rem(k + 1, per) == 0) & (flag_ref[lax.rem(lax.div(k + 1, per), n_diamonds)] == 1), 1, 0)

    def flip_of(j, width, block):
        return jnp.where(j < -width * r, left, jnp.where(j >= block - width * r, right, 0))

    for i in range(24):
        sgn[i] = jnp.where(flip_of(i - R0, 8, 32) == 1, -1.0, 1.0)
    for i in range(22):
        csgn[i] = jnp.where(flip_of(i - C0, 4, 16) == 1, -1.0, 1.0)
    for n, J in enumerate((-4, -8, -12, 4, 8, 12)):
        cflip[n] = flip_of(J, 4, 16)
    flip_l, flip_r = flip_of(-1, 8, 32), flip_of(8, 8, 32)

    lane = lax.broadcasted_iota(jnp.int32, (16, 128), 1)
    clane = lax.broadcasted_iota(jnp.int32, (8, 128), 1)
    even = lax.rem(clane, 2) == 0
    back = 127 - lane
    cback = 127 - clane

    def lo1(v):
        return jnp.where(lane == 0, 0.0, pltpu.roll(v, 1, 1))

    def hi1(v):
        return jnp.where(lane == 127, 0.0, pltpu.roll(v, 127, 1))

    def lo2(v):
        return jnp.where(clane < 2, 0.0, pltpu.roll(v, 2, 1))

    def hi2(v):
        return jnp.where(clane >= 126, 0.0, pltpu.roll(v, 126, 1))

    def landed(ref, sem):
        pltpu.make_async_copy(ref, ref, sem).wait()

    def gathered(which):
        for rt in range(4):
            @pl.when(r == rt)
            def _():
                for n in which:
                    src, dst, halo = srcs[n]
                    lo, size, at = span(rt, halo)
                    landed(cut(dst, slice(0, 4), at, size), ls.at[n])
                    landed(cut(dst, slice(0, 12), at, size), gr.at[n])
                    if rt in (0, 3):
                        landed(cut(dst, slice(0, 16), at, halo), gr.at[5 + n])

    gathered((0, 1))
    landed(rawt.at[:, pl.ds(R0, 8)], ls.at[5])
    landed(rawt.at[:, pl.ds(R0, 2 * HE)], gr.at[10])

    def put_scalars(i, turn):
        PB[i, IN] = turn(column(rawp, i))
        EB[i] = turn(column(rawe, i))
        TB[i, IN] = turn(column(rawt, i))

    def put_vector(q, i, turn):
        U[0, q, i, IN] = turn(column(rawu.at[q], i))

    def turned(flag, idx):
        return lambda v: jnp.where(flag == 1, jnp.take_along_axis(v, idx, axis=1), v)

    def put_all(put):
        rows(8, 16, lambda i: put(i, lambda v: v))
        rows(R0 - HU, R0, lambda i: put(i, turned(flip_l, back)))
        rows(R0 + 8, R0 + 8 + HU, lambda i: put(i, turned(flip_r, back)))

    put_all(put_scalars)

    def stencil(ref, s, q, i):
        v = ref[s, q, i, IN]
        total = (ref[s, q, i, UP] + ref[s, q, i, DN]) + (ref[s, q, i + 1, IN] + ref[s, q, i - 1, IN])
        return v, total + (lo1(v) + hi1(v))

    def sweep(s, q, i):
        v, total = stencil(U, s, q, i)
        U[1 - s, q, i, IN] = A * v + B * total + CB[q, i]

    def slope(ref, i, sign):
        v = ref[i, IN]
        return (ref[i, UP] - ref[i, DN], ref[i + 1, IN] - ref[i - 1, IN], sign * (hi1(v) - lo1(v)))

    def diverge(s, i, sign):
        v = U[s, 2, i, IN]
        return 0.5 * ((U[s, 0, i, UP] - U[s, 0, i, DN]) + (U[s, 1, i + 1, IN] - U[s, 1, i - 1, IN])
                      + sign * (hi1(v) - lo1(v)))

    def push(press, kinv, i):
        gr_, ga_, gb_ = slope(press, i, sgn[i])
        half = -0.5 * kinv
        CB[0, i] = kinv * (RAYLEIGH * TB[i, IN]) + half * gr_
        CB[1, i] = half * ga_
        CB[2, i] = half * gb_

    def first_push(i):
        kinv = B / EB[i]
        KB[i] = kinv
        push(PB, kinv, i)

    rows(4, 20, first_push)
    for q in range(3):
        gathered((2 + q,))
        put_all(functools.partial(put_vector, q))
        rows(4, 20, lambda i: sweep(0, q, i))
        rows(5, 19, lambda i: sweep(1, q, i))
        rows(6, 18, lambda i: sweep(0, q, i))

    halo = []
    for q in range(3):
        halo.append((remote(U.at[1, q, pl.ds(R0 + 4, 2), IN], HU_R.at[0, q], hs.at[2 * q], hr.at[2 * q], chain(1)),
                     remote(U.at[1, q, pl.ds(R0 + 2, 2), IN], HU_R.at[1, q], hs.at[2 * q + 1], hr.at[2 * q + 1], chain(-1))))
    halo.append((remote(PB.at[pl.ds(R0 + 4, 3), IN], HP_R.at[0], hs.at[6], hr.at[6], chain(1)),
                 remote(PB.at[pl.ds(R0 + 1, 3), IN], HP_R.at[1], hs.at[7], hr.at[7], chain(-1))))
    for pair in halo[:3]:
        for copy in pair:
            copy.start()

    def pre_pressure(i):
        div = diverge(1, i, sgn[i])
        DB[i] = div
        PB[i, IN] = PB[i, IN] - TAU * EB[i] * div

    rows(7, 17, pre_pressure)
    for copy in halo[3]:
        copy.start()

    def restrict(f, m, acc):
        TMP[f, m] = acc
        v = TMP[f, m, pl.ds(0, 8, stride=2)] + TMP[f, m, pl.ds(1, 8, stride=2)]
        return 0.125 * (v + jnp.where(even, pltpu.roll(v, 127, 1), pltpu.roll(v, 1, 1)))

    def pack(f, vals):
        for h in range(2):
            CS[f, h] = jnp.where(even, vals[2 * h], vals[2 * h + 1])

    def residual(q, ii):
        v, total = stencil(U, 1, q, ii)
        w = PB[ii, IN]
        if q == 0:
            gp = PB[ii, UP] - PB[ii, DN]
        elif q == 1:
            gp = PB[ii + 1, IN] - PB[ii - 1, IN]
        else:
            gp = hi1(w) - lo1(w)
        res = -0.5 * gp - EB[ii] * (6.0 * v - total)
        return res + RAYLEIGH * TB[ii, IN] if q == 0 else res

    def send_vector(q):
        one = pl.ds(q, 1)
        out = [
            remote(CS.at[one], CR.at[1, one], xs.at[q, 1], xr.at[q, 1], chain(2)),
            remote(CS.at[one], CR.at[4, one], xs.at[q, 4], xr.at[q, 4], chain(-2)),
            remote(CS.at[one, pl.ds(1, 1)], CR.at[2, one, pl.ds(1, 1)], xs.at[q, 2], xr.at[q, 2], chain(3)),
            remote(CS.at[one, pl.ds(0, 1)], CR.at[5, one, pl.ds(0, 1)], xs.at[q, 5], xr.at[q, 5], chain(-3)),
            remote(CS.at[one], CR.at[0, one], xs.at[q, 0], xr.at[q, 0], chain(1)),
            remote(CS.at[one], CR.at[3, one], xs.at[q, 3], xr.at[q, 3], chain(-1)),
        ]
        for copy in out:
            copy.start()
        return out

    ce = [restrict(3, m, EB[R0 + 2 * m] + EB[R0 + 2 * m + 1]) for m in range(4)]
    cg = [restrict(4, m, DB[R0 + 2 * m] + DB[R0 + 2 * m + 1]) for m in range(4)]
    cinv = [(4.0 * B) / e for e in ce]
    ex = []
    for q in range(3):
        vals = [cinv[m] * restrict(q, m, residual(q, R0 + 2 * m) + residual(q, R0 + 2 * m + 1)) for m in range(4)]
        pack(q, vals)
        ex.append(send_vector(q))
        for m in range(4):
            CU[0, q, C0 + m, CIN] = vals[m]
            CC[q, C0 + m] = vals[m]
    pack(3, ce)
    pack(4, cg)
    both = pl.ds(3, 2)
    ex.append([
        remote(CS.at[both, pl.ds(1, 1)], CR.at[1, both, pl.ds(1, 1)], xs.at[3, 1], xr.at[3, 1], chain(2)),
        remote(CS.at[both, pl.ds(0, 1)], CR.at[4, both, pl.ds(0, 1)], xs.at[3, 4], xr.at[3, 4], chain(-2)),
        remote(CS.at[both], CR.at[0, both], xs.at[3, 0], xr.at[3, 0], chain(1)),
        remote(CS.at[both], CR.at[3, both], xs.at[3, 3], xr.at[3, 3], chain(-1)),
    ])
    for copy in ex[3]:
        copy.start()
    for m in range(4):
        CE[C0 + m] = ce[m]
        CG[C0 + m] = cg[m]

    def unpack(x):
        return (jnp.where(even, x, pltpu.roll(x, 1, 1)), jnp.where(even, pltpu.roll(x, 127, 1), x))

    def take(n, f, h):
        turn = turned(cflip[n], cback)
        a, b = unpack(CR[n, f, h])
        return turn(a), turn(b)

    def csweep(s, q, i):
        v = CU[s, q, i, CIN]
        total = (CU[s, q, i, CUP] + CU[s, q, i, CDN]) + (CU[s, q, i + 1, CIN] + CU[s, q, i - 1, CIN])
        CU[1 - s, q, i, CIN] = A * v + B * (total + (lo2(v) + hi2(v))) + CC[q, i]

    def cdiverge(s, i):
        v = CU[s, 2, i, CIN]
        return 0.25 * ((CU[s, 0, i, CUP] - CU[s, 0, i, CDN]) + (CU[s, 1, i + 1, CIN] - CU[s, 1, i - 1, CIN])
                       + csgn[i] * (hi2(v) - lo2(v)))

    for q in range(3):
        for copy in ex[q]:
            copy.wait_recv()
        for n, base in ((0, -4), (3, 4), (1, -8), (4, 8)):
            for h in range(2):
                I = C0 + base + 2 * h
                for o, v in zip((I, I + 1), take(n, q, h)):
                    CU[0, q, o, CIN] = v
                    CC[q, o] = v
        CU[0, q, 0, CIN] = take(2, q, 1)[1]
        CU[0, q, 21, CIN] = take(5, q, 0)[0]
        rows(1, 21, lambda i: csweep(0, q, i))
        rows(2, 20, lambda i: csweep(1, q, i))

    for copy in ex[3]:
        copy.wait_recv()
    for n, I, h in ((0, -4, 0), (0, -2, 1), (3, 4, 0), (3, 6, 1), (1, -6, 1), (4, 8, 0)):
        for f, ref in ((3, CE), (4, CG)):
            ref[C0 + I], ref[C0 + I + 1] = take(n, f, h)

    def cpress1(i):
        CP[i, CIN] = -TAU * CE[i] * (cdiverge(0, i) + CG[i])

    rows(3, 19, cpress1)

    def cfirst(i):
        v = CP[i, CIN]
        scale = (-B) / CE[i]
        CC[0, i] = CC[0, i] + scale * (CP[i, CUP] - CP[i, CDN])
        CC[1, i] = CC[1, i] + scale * (CP[i + 1, CIN] - CP[i - 1, CIN])
        CC[2, i] = CC[2, i] + scale * (csgn[i] * (hi2(v) - lo2(v)))
        for q in range(3):
            csweep(0, q, i)

    rows(4, 18, cfirst)
    for q in range(3):
        rows(5, 17, lambda i: csweep(1, q, i))
    for q in range(3):
        rows(6, 16, lambda i: csweep(0, q, i))

    def spread(f, m, v):
        X[f, m, pl.ds(0, 8, stride=2)] = v
        X[f, m, pl.ds(1, 8, stride=2)] = v

    def back_up_p(i):
        spread(3, i - 7, CP[i, CIN] - TAU * CE[i] * (cdiverge(1, i) + CG[i]))

    rows(7, 15, back_up_p)
    turns = (turned(flip_l, back), turned(flip_r, back))
    for copy in halo[3]:
        copy.wait_recv()
    for side, prow in ((0, 4), (1, 17)):
        for n in range(3):
            PB[prow + n, IN] = turns[side](HP_R[side, n])

    def add_p(m):
        for n in range(2):
            PF[4 + 2 * m + n, IN] = PB[4 + 2 * m + n, IN] + X[3, m]

    rows(0, 8, add_p)
    rows(5, 19, lambda i: push(PF, KB[i], i))

    mine = pl.ds(pl.multiple_of(r * 8, 8), 8)

    def place(f):
        return uo_ref.at[f] if f < 3 else po_ref

    def home(f, step):
        rt = lax.rem(r + step, 4)
        return remote(OUT.at[f, pl.ds(4 * rt, 4)], place(f).at[:, mine], os_.at[f, step], or_.at[f], (g, d, rt))

    def own(f):
        return pltpu.make_async_copy(OUT.at[f, layers], place(f).at[:, mine], ol.at[f])

    def send_home(f):
        for step in (2, 1, 3):
            home(f, step).start()
        own(f).start()

    for q in range(3):
        for copy in halo[q]:
            copy.wait_recv()
        for side, urow in ((0, 4), (1, 18)):
            for n in range(2):
                U[1, q, urow + n, IN] = turns[side](HU_R[side, q, n])
        rows(7, 15, lambda i: spread(q, i - 7, CU[1, q, i, CIN]))

        def add_u(m):
            for n in range(2):
                U[0, q, 4 + 2 * m + n, IN] = U[1, q, 4 + 2 * m + n, IN] + X[q, m]

        rows(0, 8, add_u)
        for copy in halo[q]:
            copy.wait_send()
        rows(5, 19, lambda i: sweep(0, q, i))
        rows(6, 18, lambda i: sweep(1, q, i))
        rows(7, 17, lambda i: sweep(0, q, i))
        rows(0, 8, lambda a: set_column(OUT.at[q], a, U[1, q, R0 + a, IN]))
        send_home(q)

    def finish_p(a):
        i = R0 + a
        set_column(OUT.at[3], a, PF[i, IN] - TAU * EB[i] * diverge(1, i, 1.0))

    rows(0, 8, finish_p)
    send_home(3)

    def finish_t(a):
        i = R0 + a
        t = TB[i, IN]
        up, dn, nx, pv, hi, lo = TB[i, UP], TB[i, DN], TB[i + 1, IN], TB[i - 1, IN], hi1(t), lo1(t)
        lap = 6.0 * t - (((up + dn) + (nx + pv)) + (hi + lo))
        carried = 0.5 * (U[1, 0, i, IN] * (up - dn) + U[1, 1, i, IN] * (nx - pv) + U[1, 2, i, IN] * (hi - lo))
        set_column(to_ref, a, t + TIME_STEP * (-KAPPA * lap - carried))

    rows(0, 8, finish_t)

    for copy in halo[3]:
        copy.wait_send()
    for copy in heat:
        copy.wait_send()
    for n in range(5):
        for copy in lateral(n):
            copy.wait_send()
    for group in ex:
        for copy in group:
            copy.wait_send()
    for rt in range(4):
        @pl.when(r != rt)
        def _():
            for n in range(5):
                across(n, rt).wait_send()
    for f in range(4):
        for step in (2, 1, 3):
            home(f, step).wait_send()
        own(f).wait()
    for f in range(4):
        landed(place(f).at[:, pl.ds(0, 24)], or_.at[f])


def write_out(*refs):
    sem = refs[6]
    copies = [pltpu.make_async_copy(refs[n], refs[3 + n], sem.at[n]) for n in range(3)]
    for copy in copies:
        copy.start()
    for copy in copies:
        copy.wait()


def per_device(n_dia, n_chain, t, u, p, e, flags):
    f32 = jnp.float32
    V = pltpu.VMEM
    DMA = pltpu.SemaphoreType.DMA
    any_ = pl.BlockSpec(memory_space=pl.ANY)
    vmem = pl.BlockSpec(memory_space=pltpu.VMEM)
    done = pl.pallas_call(
        functools.partial(kernel, n_dia, n_chain, flags.shape[0]),
        out_shape=(
            V(u.shape, f32),
            V(p.shape, f32),
            V(t.shape, f32),
        ),
        in_specs=[any_] * 5,
        out_specs=(vmem,) * 3,
        scratch_shapes=[
            V((3, 16, 24, 128), f32), V((16, 24, 128), f32), V((16, 24, 128), f32), V((16, 24, 128), f32),
            V((2, 3, 24, 32, 128), f32), V((24, 32, 128), f32), V((24, 32, 128), f32),
            V((24, 16, 128), f32), V((24, 16, 128), f32), V((24, 32, 128), f32),
            V((3, 24, 16, 128), f32), V((24, 16, 128), f32), V((5, 4, 16, 128), f32),
            V((5, 2, 8, 128), f32), V((6, 5, 2, 8, 128), f32),
            V((2, 3, 22, 24, 128), f32), V((3, 22, 8, 128), f32), V((22, 8, 128), f32), V((22, 8, 128), f32),
            V((22, 24, 128), f32), V((4, 8, 16, 128), f32),
            V((2, 3, 2, 16, 128), f32), V((2, 3, 16, 128), f32),
            V((4, 16, 8, 128), f32),
            pltpu.SMEM(flags.shape, jnp.int32), pltpu.SMEM((24,), f32), pltpu.SMEM((22,), f32), pltpu.SMEM((6,), jnp.int32),
            DMA((6, 6)), DMA((11,)), DMA((6,)), DMA((8,)), DMA((8,)), DMA((4, 6)), DMA((4, 6)),
            DMA((4, 4)), DMA((4,)), DMA((4,)), DMA,
        ],
        compiler_params=pltpu.CompilerParams(collective_id=0, has_side_effects=True),
        name="cycle",
    )(t, u, p, e, flags)
    return pl.pallas_call(
        write_out,
        out_shape=[jax.ShapeDtypeStruct(x.shape, f32) for x in done],
        in_specs=[vmem] * 3,
        out_specs=[any_] * 3,
        scratch_shapes=[DMA((3,))],
        name="write_out",
    )(*[pltpu.with_memory_space_constraint(x, pltpu.VMEM) for x in done])


def solution(mesh):
    n_dia = mesh.shape["dia"]
    n_chain = n_dia * mesh.shape["grp"] * mesh.shape["rad"]
    return jax.shard_map(
        functools.partial(per_device, n_dia, n_chain),
        mesh=mesh,
        in_specs=(
            P(None, ("grp", "dia", "rad"), None),
            P(None, "rad", ("grp", "dia"), None),
            P("rad", ("grp", "dia"), None),
            P("rad", ("grp", "dia"), None),
            P(),
        ),
        out_specs=(
            P(None, "rad", ("grp", "dia"), None),
            P("rad", ("grp", "dia"), None),
            P(None, ("grp", "dia", "rad"), None),
        ),
        check_vma=False,
    )
```

time: 39 us -> 37.2 us (0.954)
  Pallas kernels: 38.3 us -> 36.5 us
    pallas_call x1, Pallas kernels: 37.5 us -> 35.7 us  [per_device(): pl.pallas_call(functools.partial(kernel, n_dia, n_chain, flags.shape[0]),...]
where the time goes in v2:
time: 37.2 us; the launch traced here: 37.1 us
  Pallas kernels  36.5 us (98%)
  between operations  0.64 us (2%)
    pallas_call x1, Pallas kernels, per_device(): pl.pallas_call(functools.partial(kernel, n_dia, n_chain, flags.shape[0]),...  35.7 us
    pallas_call x1, Pallas kernels, per_device(): pl.pallas_call(write_out, out_shape=[jax.ShapeDtypeStruct(x.shape, f32) f...  0.74 us

profile of v2, /device:TPU:1, one launch (start us, length us, event | category | flops | bytes accessed | tf_op | source)
XLA Modules:
  0.0 37.1 jit_solution(9930892711109443624)
XLA Ops:
  0.6 35.7 %cycle.1 = (f32[3,4,32,128]{3,2,1,0:T(8,128)S(1)}, f32[4,32,128]{2,1,0:T(8,128)S(1)}, f32[16,8,128]{2,1,0:T(8,128)S(1)}) custom-call(f32[16,8,128]{2,1,0:T(8,128)} %t_ref.1, f32[3,4,32,128]{3,2,1,0:T(8,128)} %u_ref.1, f32[4,32,128]{2,1,0:T(8,128)} %p_ref.1, f32[4,32,128]{2,1,0:T(8,128)} %e_ref.1, s32[16]{0:T(128)} %flag_hbm.1), custom_call_target="tpu_custom_call" | custom-call | tf_op jit(solution)/shard_map/cycle/pallas_call | solution.py:521
  36.4 0.7 %write_out.1 = (f32[3,4,32,128]{3,2,1,0:T(8,128)}, f32[4,32,128]{2,1,0:T(8,128)}, f32[16,8,128]{2,1,0:T(8,128)}) custom-call(f32[3,4,32,128]{3,2,1,0:T(8,128)S(1)} %get-tuple-element.6.refs_0_, f32[4,32,128]{2,1,0:T(8,128)S(1)} %get-tuple-element.7.refs_1_, f32[16,8,128]{2,1,0:T(8,128)S(1)} %get-tuple-element.8.refs_2_), custom_call_target="tpu_custom_call" | custom-call | tf_op jit(solution)/shard_map/write_out/pallas_call | solution.py:547

commit v3 on v2

--- a/solution.py
+++ b/solution.py
@@ -113,14 +113,14 @@
     for rs in range(4):
         @pl.when(r == rs)
         def _():
+            for copy in heat:
+                copy.start()
             for n in range(5):
                 for copy in lateral(n):
                     copy.start()
+            for n in range(5):
                 for step in (2, 1, 3):
                     across(n, (rs + step) % 4).start()
-                if n == 1:
-                    for copy in heat:
-                        copy.start()
 
     read_flags = pltpu.make_async_copy(flag_hbm, flag_ref, fs)
     read_flags.start()
@@ -271,9 +271,6 @@
                      remote(U.at[1, q, pl.ds(R0 + 2, 2), IN], HU_R.at[1, q], hs.at[2 * q + 1], hr.at[2 * q + 1], chain(-1))))
     halo.append((remote(PB.at[pl.ds(R0 + 4, 3), IN], HP_R.at[0], hs.at[6], hr.at[6], chain(1)),
                  remote(PB.at[pl.ds(R0 + 1, 3), IN], HP_R.at[1], hs.at[7], hr.at[7], chain(-1))))
-    for pair in halo[:3]:
-        for copy in pair:
-            copy.start()
 
     def pre_pressure(i):
         div = diverge(1, i, sgn[i])
@@ -341,6 +338,9 @@
     ])
     for copy in ex[3]:
         copy.start()
+    for pair in halo[:3]:
+        for copy in pair:
+            copy.start()
     for m in range(4):
         CE[C0 + m] = ce[m]
         CG[C0 + m] = cg[m]

time: 37.2 us -> 36.3 us (0.976)
  Pallas kernels: 36.5 us -> 35.5 us
    pallas_call x1, Pallas kernels: 35.7 us -> 34.8 us  [per_device(): pl.pallas_call(functools.partial(kernel, n_dia, n_chain, flags.shape[0]),...]
where the time goes in v3:
time: 36.3 us; the launch traced here: 36.2 us
  Pallas kernels  35.5 us (98%)
  between operations  0.64 us (2%)
    pallas_call x1, Pallas kernels, per_device(): pl.pallas_call(functools.partial(kernel, n_dia, n_chain, flags.shape[0]),...  34.8 us
    pallas_call x1, Pallas kernels, per_device(): pl.pallas_call(write_out, out_shape=[jax.ShapeDtypeStruct(x.shape, f32) f...  0.74 us

profile of v3, /device:TPU:1, one launch (start us, length us, event | category | flops | bytes accessed | tf_op | source)
XLA Modules:
  0.0 36.2 jit_solution(6230869019735879217)
XLA Ops:
  0.6 34.8 %cycle.1 = (f32[3,4,32,128]{3,2,1,0:T(8,128)S(1)}, f32[4,32,128]{2,1,0:T(8,128)S(1)}, f32[16,8,128]{2,1,0:T(8,128)S(1)}) custom-call(f32[16,8,128]{2,1,0:T(8,128)} %t_ref.1, f32[3,4,32,128]{3,2,1,0:T(8,128)} %u_ref.1, f32[4,32,128]{2,1,0:T(8,128)} %p_ref.1, f32[4,32,128]{2,1,0:T(8,128)} %e_ref.1, s32[16]{0:T(128)} %flag_hbm.1), custom_call_target="tpu_custom_call" | custom-call | tf_op jit(solution)/shard_map/cycle/pallas_call | solution.py:521
  35.4 0.7 %write_out.1 = (f32[3,4,32,128]{3,2,1,0:T(8,128)}, f32[4,32,128]{2,1,0:T(8,128)}, f32[16,8,128]{2,1,0:T(8,128)}) custom-call(f32[3,4,32,128]{3,2,1,0:T(8,128)S(1)} %get-tuple-element.6.refs_0_, f32[4,32,128]{2,1,0:T(8,128)S(1)} %get-tuple-element.7.refs_1_, f32[16,8,128]{2,1,0:T(8,128)S(1)} %get-tuple-element.8.refs_2_), custom_call_target="tpu_custom_call" | custom-call | tf_op jit(solution)/shard_map/write_out/pallas_call | solution.py:547

commit v4 on v3

--- a/solution.py
+++ b/solution.py
@@ -57,27 +57,47 @@
     U, PB, PF, EB, KB, TB, CB, DB, TMP,
     CS, CR, CU, CC, CE, CG, CP, X, HU_R, HP_R, OUT,
     flag_ref, sgn, csgn, cflip,
-    gs, gr, ls, hs, hr, xs, xr, os_, or_, ol, fs,
+    gs, gr, ls, hs, hr, xs, xr, os_, or_, ol, fs, go,
 ):
     g = lax.axis_index("grp")
     d = lax.axis_index("dia")
     r = lax.axis_index("rad")
     k = g * n_dia + d
-    c = k * 4 + r
     n_k = n_chain // 4
-
-    def dev(ci):
-        kk = lax.div(ci, 4)
-        return (lax.div(kk, n_dia), lax.rem(kk, n_dia), lax.rem(ci, 4))
+    n_grp = n_k // n_dia
+
+    over = d == n_dia - 1
+    under = d == 0
+    next_g = jnp.where(over, jnp.where(g == n_grp - 1, 0, g + 1), g)
+    next_d = jnp.where(over, 0, d + 1)
+    prev_g = jnp.where(under, jnp.where(g == 0, n_grp - 1, g - 1), g)
+    prev_d = jnp.where(under, n_dia - 1, d - 1)
+    to_next, to_prev = (next_g, next_d, 0), (prev_g, prev_d, 3)
+    chains = {4: (next_g, next_d, r), -4: (prev_g, prev_d, r)}
+    for step in (1, 2, 3):
+        out = r + step >= 4
+        chains[step] = (jnp.where(out, next_g, g), jnp.where(out, next_d, d), jnp.where(out, r + step - 4, r + step))
+        out = r - step < 0
+        chains[-step] = (jnp.where(out, prev_g, g), jnp.where(out, prev_d, d), jnp.where(out, r - step + 4, r - step))
 
     def chain(step):
-        return dev(lax.rem(c + step + n_chain, n_chain))
+        return chains[step]
+
+    def signal(sem, to):
+        pl.semaphore_signal(sem, inc=1, device_id=to, device_id_type=MESH)
 
     barrier = pltpu.get_barrier_semaphore()
-    for step in (1, -1, 2, -2, 3, -3, 4, -4):
-        pl.semaphore_signal(barrier, inc=1, device_id=chain(step), device_id_type=MESH)
-
-    pl.semaphore_wait(barrier, 8)
+    for step in (1, 2, 3):
+        signal(barrier, (g, d, jnp.where(r + step >= 4, r + step - 4, r + step)))
+    for step in (1, 2, 3, 4):
+        @pl.when(r - step < 0)
+        def _():
+            signal(barrier, chain(-step))
+    pl.semaphore_wait(barrier, r + 4)
+    for step in (1, 2, 3, 4):
+        @pl.when(r + step >= 4)
+        def _():
+            signal(go, chain(step))
 
     layers = pl.ds(r * 4, 4)
     srcs = ((p_ref, rawp, HU), (e_ref, rawe, HE)) + tuple((u_ref.at[q], rawu.at[q], HU) for q in range(3))
@@ -88,11 +108,6 @@
     def remote(src, dst, ssem, rsem, to):
         return pltpu.make_async_remote_copy(
             src_ref=src, dst_ref=dst, send_sem=ssem, recv_sem=rsem, device_id=to, device_id_type=MESH)
-
-    nxt = lax.rem(k + 1, n_k)
-    prv = lax.rem(k - 1 + n_k, n_k)
-    to_next = (lax.div(nxt, n_dia), lax.rem(nxt, n_dia), 0)
-    to_prev = (lax.div(prv, n_dia), lax.rem(prv, n_dia), 3)
 
     def lateral(n):
         src, dst, halo = srcs[n]
@@ -110,17 +125,18 @@
     heat = [
         remote(t_ref.at[:, pl.ds(8 - HE, HE)], rawt.at[:, pl.ds(R0 - HE, HE)], gs.at[5, 0], gr.at[10], chain(1)),
         remote(t_ref.at[:, pl.ds(0, HE)], rawt.at[:, pl.ds(R0 + 8, HE)], gs.at[5, 1], gr.at[10], chain(-1))]
-    for rs in range(4):
-        @pl.when(r == rs)
-        def _():
-            for copy in heat:
-                copy.start()
-            for n in range(5):
-                for copy in lateral(n):
-                    copy.start()
-            for n in range(5):
-                for step in (2, 1, 3):
-                    across(n, (rs + step) % 4).start()
+    def send_across(fields):
+        for rs in range(4):
+            @pl.when(r == rs)
+            def _():
+                for n in fields:
+                    for step in (2, 1, 3):
+                        across(n, (rs + step) % 4).start()
+
+    heat[0].start()
+    for n in range(5):
+        lateral(n)[0].start()
+    send_across((0, 1))
 
     read_flags = pltpu.make_async_copy(flag_hbm, flag_ref, fs)
     read_flags.start()
@@ -154,6 +170,11 @@
         CP[i, pl.ds(16, 8)] = z
 
     rows(0, 22, cclear, 1)
+    pl.semaphore_wait(go, 4 - r)
+    heat[1].start()
+    for n in range(5):
+        lateral(n)[1].start()
+    send_across((2, 3, 4))
 
     read_flags.wait()
     per = DIA_ROWS // 32
@@ -236,30 +257,59 @@
         v, total = stencil(U, s, q, i)
         U[1 - s, q, i, IN] = A * v + B * total + CB[q, i]
 
-    def slope(ref, i, sign):
-        v = ref[i, IN]
-        return (ref[i, UP] - ref[i, DN], ref[i + 1, IN] - ref[i - 1, IN], sign * (hi1(v) - lo1(v)))
-
     def diverge(s, i, sign):
         v = U[s, 2, i, IN]
         return 0.5 * ((U[s, 0, i, UP] - U[s, 0, i, DN]) + (U[s, 1, i + 1, IN] - U[s, 1, i - 1, IN])
                       + sign * (hi1(v) - lo1(v)))
 
-    def push(press, kinv, i):
-        gr_, ga_, gb_ = slope(press, i, sgn[i])
+    def push(press, kinv, q, i):
         half = -0.5 * kinv
-        CB[0, i] = kinv * (RAYLEIGH * TB[i, IN]) + half * gr_
-        CB[1, i] = half * ga_
-        CB[2, i] = half * gb_
+        if q == 0:
+            CB[0, i] = kinv * (RAYLEIGH * TB[i, IN]) + half * (press[i, UP] - press[i, DN])
+        elif q == 1:
+            CB[1, i] = half * (press[i + 1, IN] - press[i - 1, IN])
+        else:
+            v = press[i, IN]
+            CB[2, i] = half * (sgn[i] * (hi1(v) - lo1(v)))
 
     def first_push(i):
         kinv = B / EB[i]
         KB[i] = kinv
-        push(PB, kinv, i)
+        for q in range(3):
+            push(PB, kinv, q, i)
 
     rows(4, 20, first_push)
+    def restrict(f, m, acc):
+        TMP[f, m] = acc
+        v = TMP[f, m, pl.ds(0, 8, stride=2)] + TMP[f, m, pl.ds(1, 8, stride=2)]
+        return 0.125 * (v + jnp.where(even, pltpu.roll(v, 127, 1), pltpu.roll(v, 1, 1)))
+
+    def pack(f, vals):
+        for h in range(2):
+            CS[f, h] = jnp.where(even, vals[2 * h], vals[2 * h + 1])
+
+    def send_scalar(f):
+        one = pl.ds(f, 1)
+        out = [
+            remote(CS.at[one, pl.ds(1, 1)], CR.at[1, one, pl.ds(1, 1)], xs.at[f, 1], xr.at[f, 1], chain(2)),
+            remote(CS.at[one, pl.ds(0, 1)], CR.at[4, one, pl.ds(0, 1)], xs.at[f, 4], xr.at[f, 4], chain(-2)),
+            remote(CS.at[one], CR.at[0, one], xs.at[f, 0], xr.at[f, 0], chain(1)),
+            remote(CS.at[one], CR.at[3, one], xs.at[f, 3], xr.at[f, 3], chain(-1)),
+        ]
+        for copy in out:
+            copy.start()
+        return out
+
+    ce = [restrict(3, m, EB[R0 + 2 * m] + EB[R0 + 2 * m + 1]) for m in range(4)]
+    cinv = [(4.0 * B) / e for e in ce]
+    pack(3, ce)
+    for m in range(4):
+        CE[C0 + m] = ce[m]
+
     for q in range(3):
         gathered((2 + q,))
+        if q == 2:
+            ex_e = send_scalar(3)
         put_all(functools.partial(put_vector, q))
         rows(4, 20, lambda i: sweep(0, q, i))
         rows(5, 19, lambda i: sweep(1, q, i))
@@ -278,17 +328,6 @@
         PB[i, IN] = PB[i, IN] - TAU * EB[i] * div
 
     rows(7, 17, pre_pressure)
-    for copy in halo[3]:
-        copy.start()
-
-    def restrict(f, m, acc):
-        TMP[f, m] = acc
-        v = TMP[f, m, pl.ds(0, 8, stride=2)] + TMP[f, m, pl.ds(1, 8, stride=2)]
-        return 0.125 * (v + jnp.where(even, pltpu.roll(v, 127, 1), pltpu.roll(v, 1, 1)))
-
-    def pack(f, vals):
-        for h in range(2):
-            CS[f, h] = jnp.where(even, vals[2 * h], vals[2 * h + 1])
 
     def residual(q, ii):
         v, total = stencil(U, 1, q, ii)
@@ -306,19 +345,16 @@
         one = pl.ds(q, 1)
         out = [
             remote(CS.at[one], CR.at[1, one], xs.at[q, 1], xr.at[q, 1], chain(2)),
+            remote(CS.at[one, pl.ds(1, 1)], CR.at[2, one, pl.ds(1, 1)], xs.at[q, 2], xr.at[q, 2], chain(3)),
+            remote(CS.at[one], CR.at[0, one], xs.at[q, 0], xr.at[q, 0], chain(1)),
             remote(CS.at[one], CR.at[4, one], xs.at[q, 4], xr.at[q, 4], chain(-2)),
-            remote(CS.at[one, pl.ds(1, 1)], CR.at[2, one, pl.ds(1, 1)], xs.at[q, 2], xr.at[q, 2], chain(3)),
             remote(CS.at[one, pl.ds(0, 1)], CR.at[5, one, pl.ds(0, 1)], xs.at[q, 5], xr.at[q, 5], chain(-3)),
-            remote(CS.at[one], CR.at[0, one], xs.at[q, 0], xr.at[q, 0], chain(1)),
             remote(CS.at[one], CR.at[3, one], xs.at[q, 3], xr.at[q, 3], chain(-1)),
         ]
         for copy in out:
             copy.start()
         return out
 
-    ce = [restrict(3, m, EB[R0 + 2 * m] + EB[R0 + 2 * m + 1]) for m in range(4)]
-    cg = [restrict(4, m, DB[R0 + 2 * m] + DB[R0 + 2 * m + 1]) for m in range(4)]
-    cinv = [(4.0 * B) / e for e in ce]
     ex = []
     for q in range(3):
         vals = [cinv[m] * restrict(q, m, residual(q, R0 + 2 * m) + residual(q, R0 + 2 * m + 1)) for m in range(4)]
@@ -327,22 +363,13 @@
         for m in range(4):
             CU[0, q, C0 + m, CIN] = vals[m]
             CC[q, C0 + m] = vals[m]
-    pack(3, ce)
+    cg = [restrict(4, m, DB[R0 + 2 * m] + DB[R0 + 2 * m + 1]) for m in range(4)]
     pack(4, cg)
-    both = pl.ds(3, 2)
-    ex.append([
-        remote(CS.at[both, pl.ds(1, 1)], CR.at[1, both, pl.ds(1, 1)], xs.at[3, 1], xr.at[3, 1], chain(2)),
-        remote(CS.at[both, pl.ds(0, 1)], CR.at[4, both, pl.ds(0, 1)], xs.at[3, 4], xr.at[3, 4], chain(-2)),
-        remote(CS.at[both], CR.at[0, both], xs.at[3, 0], xr.at[3, 0], chain(1)),
-        remote(CS.at[both], CR.at[3, both], xs.at[3, 3], xr.at[3, 3], chain(-1)),
-    ])
-    for copy in ex[3]:
-        copy.start()
-    for pair in halo[:3]:
+    ex.append(ex_e + send_scalar(4))
+    for pair in (halo[3],) + tuple(halo[:3]):
         for copy in pair:
             copy.start()
     for m in range(4):
-        CE[C0 + m] = ce[m]
         CG[C0 + m] = cg[m]
 
     def unpack(x):
@@ -423,7 +450,6 @@
             PF[4 + 2 * m + n, IN] = PB[4 + 2 * m + n, IN] + X[3, m]
 
     rows(0, 8, add_p)
-    rows(5, 19, lambda i: push(PF, KB[i], i))
 
     mine = pl.ds(pl.multiple_of(r * 8, 8), 8)
 
@@ -431,7 +457,7 @@
         return uo_ref.at[f] if f < 3 else po_ref
 
     def home(f, step):
-        rt = lax.rem(r + step, 4)
+        rt = jnp.where(r + step >= 4, r + step - 4, r + step)
         return remote(OUT.at[f, pl.ds(4 * rt, 4)], place(f).at[:, mine], os_.at[f, step], or_.at[f], (g, d, rt))
 
     def own(f):
@@ -457,6 +483,7 @@
         rows(0, 8, add_u)
         for copy in halo[q]:
             copy.wait_send()
+        rows(5, 19, lambda i: push(PF, KB[i], q, i))
         rows(5, 19, lambda i: sweep(0, q, i))
         rows(6, 18, lambda i: sweep(1, q, i))
         rows(7, 17, lambda i: sweep(0, q, i))
@@ -538,8 +565,8 @@
             V((2, 3, 2, 16, 128), f32), V((2, 3, 16, 128), f32),
             V((4, 16, 8, 128), f32),
             pltpu.SMEM(flags.shape, jnp.int32), pltpu.SMEM((24,), f32), pltpu.SMEM((22,), f32), pltpu.SMEM((6,), jnp.int32),
-            DMA((6, 6)), DMA((11,)), DMA((6,)), DMA((8,)), DMA((8,)), DMA((4, 6)), DMA((4, 6)),
-            DMA((4, 4)), DMA((4,)), DMA((4,)), DMA,
+            DMA((6, 6)), DMA((11,)), DMA((6,)), DMA((8,)), DMA((8,)), DMA((5, 6)), DMA((5, 6)),
+            DMA((4, 4)), DMA((4,)), DMA((4,)), DMA, pltpu.SemaphoreType.REGULAR,
         ],
         compiler_params=pltpu.CompilerParams(collective_id=0, has_side_effects=True),
         name="cycle",

time: 36.3 us -> 36.1 us (level)
  no operation moved by 1% of the time
where the time goes in v4:
time: 36.1 us; the launch traced here: 36 us
  Pallas kernels  35.3 us (98%)
  between operations  0.64 us (2%)
    pallas_call x1, Pallas kernels, per_device(): pl.pallas_call(functools.partial(kernel, n_dia, n_chain, flags.shape[0]),...  34.6 us
    pallas_call x1, Pallas kernels, per_device(): pl.pallas_call(write_out, out_shape=[jax.ShapeDtypeStruct(x.shape, f32) f...  0.74 us

profile of v4, /device:TPU:1, one launch (start us, length us, event | category | flops | bytes accessed | tf_op | source)
XLA Modules:
  0.0 36.0 jit_solution(11544303278981815824)
XLA Ops:
  0.6 34.6 %cycle.1 = (f32[3,4,32,128]{3,2,1,0:T(8,128)S(1)}, f32[4,32,128]{2,1,0:T(8,128)S(1)}, f32[16,8,128]{2,1,0:T(8,128)S(1)}) custom-call(f32[16,8,128]{2,1,0:T(8,128)} %t_ref.1, f32[3,4,32,128]{3,2,1,0:T(8,128)} %u_ref.1, f32[4,32,128]{2,1,0:T(8,128)} %p_ref.1, f32[4,32,128]{2,1,0:T(8,128)} %e_ref.1, s32[16]{0:T(128)} %flag_hbm.1), custom_call_target="tpu_custom_call" | custom-call | tf_op jit(solution)/shard_map/cycle/pallas_call | solution.py:548
  35.2 0.7 %write_out.1 = (f32[3,4,32,128]{3,2,1,0:T(8,128)}, f32[4,32,128]{2,1,0:T(8,128)}, f32[16,8,128]{2,1,0:T(8,128)}) custom-call(f32[3,4,32,128]{3,2,1,0:T(8,128)S(1)} %get-tuple-element.6.refs_0_, f32[4,32,128]{2,1,0:T(8,128)S(1)} %get-tuple-element.7.refs_1_, f32[16,8,128]{2,1,0:T(8,128)S(1)} %get-tuple-element.8.refs_2_), custom_call_target="tpu_custom_call" | custom-call | tf_op jit(solution)/shard_map/write_out/pallas_call | solution.py:574

commit v5 on v3

--- a/solution.py
+++ b/solution.py
@@ -278,8 +278,6 @@
         PB[i, IN] = PB[i, IN] - TAU * EB[i] * div
 
     rows(7, 17, pre_pressure)
-    for copy in halo[3]:
-        copy.start()
 
     def restrict(f, m, acc):
         TMP[f, m] = acc
@@ -338,7 +336,7 @@
     ])
     for copy in ex[3]:
         copy.start()
-    for pair in halo[:3]:
+    for pair in (halo[3],) + tuple(halo[:3]):
         for copy in pair:
             copy.start()
     for m in range(4):

time: 36.3 us -> 36.2 us (level)
  no operation moved by 1% of the time
where the time goes in v5:
time: 36.2 us; the launch traced here: 36.1 us
  Pallas kernels  35.5 us (98%)
  between operations  0.64 us (2%)
    pallas_call x1, Pallas kernels, per_device(): pl.pallas_call(functools.partial(kernel, n_dia, n_chain, flags.shape[0]),...  34.7 us
    pallas_call x1, Pallas kernels, per_device(): pl.pallas_call(write_out, out_shape=[jax.ShapeDtypeStruct(x.shape, f32) f...  0.74 us

profile of v5, /device:TPU:1, one launch (start us, length us, event | category | flops | bytes accessed | tf_op | source)
XLA Modules:
  0.0 36.1 jit_solution(10283884964439690153)
XLA Ops:
  0.6 34.7 %cycle.1 = (f32[3,4,32,128]{3,2,1,0:T(8,128)S(1)}, f32[4,32,128]{2,1,0:T(8,128)S(1)}, f32[16,8,128]{2,1,0:T(8,128)S(1)}) custom-call(f32[16,8,128]{2,1,0:T(8,128)} %t_ref.1, f32[3,4,32,128]{3,2,1,0:T(8,128)} %u_ref.1, f32[4,32,128]{2,1,0:T(8,128)} %p_ref.1, f32[4,32,128]{2,1,0:T(8,128)} %e_ref.1, s32[16]{0:T(128)} %flag_hbm.1), custom_call_target="tpu_custom_call" | custom-call | tf_op jit(solution)/shard_map/cycle/pallas_call | solution.py:519
  35.4 0.7 %write_out.1 = (f32[3,4,32,128]{3,2,1,0:T(8,128)}, f32[4,32,128]{2,1,0:T(8,128)}, f32[16,8,128]{2,1,0:T(8,128)}) custom-call(f32[3,4,32,128]{3,2,1,0:T(8,128)S(1)} %get-tuple-element.6.refs_0_, f32[4,32,128]{2,1,0:T(8,128)S(1)} %get-tuple-element.7.refs_1_, f32[16,8,128]{2,1,0:T(8,128)S(1)} %get-tuple-element.8.refs_2_), custom_call_target="tpu_custom_call" | custom-call | tf_op jit(solution)/shard_map/write_out/pallas_call | solution.py:545

commit v6 on v4

--- a/solution.py
+++ b/solution.py
@@ -57,7 +57,7 @@
     U, PB, PF, EB, KB, TB, CB, DB, TMP,
     CS, CR, CU, CC, CE, CG, CP, X, HU_R, HP_R, OUT,
     flag_ref, sgn, csgn, cflip,
-    gs, gr, ls, hs, hr, xs, xr, os_, or_, ol, fs, go,
+    gs, gr, ls, hs, hr, xs, xr, os_, or_, ol, fs,
 ):
     g = lax.axis_index("grp")
     d = lax.axis_index("dia")
@@ -83,21 +83,11 @@
     def chain(step):
         return chains[step]
 
-    def signal(sem, to):
-        pl.semaphore_signal(sem, inc=1, device_id=to, device_id_type=MESH)
-
     barrier = pltpu.get_barrier_semaphore()
-    for step in (1, 2, 3):
-        signal(barrier, (g, d, jnp.where(r + step >= 4, r + step - 4, r + step)))
-    for step in (1, 2, 3, 4):
-        @pl.when(r - step < 0)
-        def _():
-            signal(barrier, chain(-step))
-    pl.semaphore_wait(barrier, r + 4)
-    for step in (1, 2, 3, 4):
-        @pl.when(r + step >= 4)
-        def _():
-            signal(go, chain(step))
+    for step in (1, -1, 2, -2, 3, -3, 4, -4):
+        pl.semaphore_signal(barrier, inc=1, device_id=chain(step), device_id_type=MESH)
+
+    pl.semaphore_wait(barrier, 8)
 
     layers = pl.ds(r * 4, 4)
     srcs = ((p_ref, rawp, HU), (e_ref, rawe, HE)) + tuple((u_ref.at[q], rawu.at[q], HU) for q in range(3))
@@ -125,18 +115,17 @@
     heat = [
         remote(t_ref.at[:, pl.ds(8 - HE, HE)], rawt.at[:, pl.ds(R0 - HE, HE)], gs.at[5, 0], gr.at[10], chain(1)),
         remote(t_ref.at[:, pl.ds(0, HE)], rawt.at[:, pl.ds(R0 + 8, HE)], gs.at[5, 1], gr.at[10], chain(-1))]
-    def send_across(fields):
-        for rs in range(4):
-            @pl.when(r == rs)
-            def _():
-                for n in fields:
-                    for step in (2, 1, 3):
-                        across(n, (rs + step) % 4).start()
-
-    heat[0].start()
-    for n in range(5):
-        lateral(n)[0].start()
-    send_across((0, 1))
+    for rs in range(4):
+        @pl.when(r == rs)
+        def _():
+            for copy in heat:
+                copy.start()
+            for n in range(5):
+                for copy in lateral(n):
+                    copy.start()
+            for n in range(5):
+                for step in (2, 1, 3):
+                    across(n, (rs + step) % 4).start()
 
     read_flags = pltpu.make_async_copy(flag_hbm, flag_ref, fs)
     read_flags.start()
@@ -170,11 +159,6 @@
         CP[i, pl.ds(16, 8)] = z
 
     rows(0, 22, cclear, 1)
-    pl.semaphore_wait(go, 4 - r)
-    heat[1].start()
-    for n in range(5):
-        lateral(n)[1].start()
-    send_across((2, 3, 4))
 
     read_flags.wait()
     per = DIA_ROWS // 32
@@ -345,10 +329,10 @@
         one = pl.ds(q, 1)
         out = [
             remote(CS.at[one], CR.at[1, one], xs.at[q, 1], xr.at[q, 1], chain(2)),
+            remote(CS.at[one], CR.at[4, one], xs.at[q, 4], xr.at[q, 4], chain(-2)),
             remote(CS.at[one, pl.ds(1, 1)], CR.at[2, one, pl.ds(1, 1)], xs.at[q, 2], xr.at[q, 2], chain(3)),
+            remote(CS.at[one, pl.ds(0, 1)], CR.at[5, one, pl.ds(0, 1)], xs.at[q, 5], xr.at[q, 5], chain(-3)),
             remote(CS.at[one], CR.at[0, one], xs.at[q, 0], xr.at[q, 0], chain(1)),
-            remote(CS.at[one], CR.at[4, one], xs.at[q, 4], xr.at[q, 4], chain(-2)),
-            remote(CS.at[one, pl.ds(0, 1)], CR.at[5, one, pl.ds(0, 1)], xs.at[q, 5], xr.at[q, 5], chain(-3)),
             remote(CS.at[one], CR.at[3, one], xs.at[q, 3], xr.at[q, 3], chain(-1)),
         ]
         for copy in out:
@@ -566,7 +550,7 @@
             V((4, 16, 8, 128), f32),
             pltpu.SMEM(flags.shape, jnp.int32), pltpu.SMEM((24,), f32), pltpu.SMEM((22,), f32), pltpu.SMEM((6,), jnp.int32),
             DMA((6, 6)), DMA((11,)), DMA((6,)), DMA((8,)), DMA((8,)), DMA((5, 6)), DMA((5, 6)),
-            DMA((4, 4)), DMA((4,)), DMA((4,)), DMA, pltpu.SemaphoreType.REGULAR,
+            DMA((4, 4)), DMA((4,)), DMA((4,)), DMA,
         ],
         compiler_params=pltpu.CompilerParams(collective_id=0, has_side_effects=True),
         name="cycle",

time: 36.1 us -> 36.1 us (level)
  no operation moved by 1% of the time
where the time goes in v6:
time: 36.1 us; the launch traced here: 36 us
  Pallas kernels  35.3 us (98%)
  between operations  0.64 us (2%)
    pallas_call x1, Pallas kernels, per_device(): pl.pallas_call(functools.partial(kernel, n_dia, n_chain, flags.shape[0]),...  34.6 us
    pallas_call x1, Pallas kernels, per_device(): pl.pallas_call(write_out, out_shape=[jax.ShapeDtypeStruct(x.shape, f32) f...  0.74 us

profile of v6, /device:TPU:1, one launch (start us, length us, event | category | flops | bytes accessed | tf_op | source)
XLA Modules:
  0.0 36.0 jit_solution(16300969812297975236)
XLA Ops:
  0.6 34.6 %cycle.1 = (f32[3,4,32,128]{3,2,1,0:T(8,128)S(1)}, f32[4,32,128]{2,1,0:T(8,128)S(1)}, f32[16,8,128]{2,1,0:T(8,128)S(1)}) custom-call(f32[16,8,128]{2,1,0:T(8,128)} %t_ref.1, f32[3,4,32,128]{3,2,1,0:T(8,128)} %u_ref.1, f32[4,32,128]{2,1,0:T(8,128)} %p_ref.1, f32[4,32,128]{2,1,0:T(8,128)} %e_ref.1, s32[16]{0:T(128)} %flag_hbm.1), custom_call_target="tpu_custom_call" | custom-call | tf_op jit(solution)/shard_map/cycle/pallas_call | solution.py:532
  35.2 0.7 %write_out.1 = (f32[3,4,32,128]{3,2,1,0:T(8,128)}, f32[4,32,128]{2,1,0:T(8,128)}, f32[16,8,128]{2,1,0:T(8,128)}) custom-call(f32[3,4,32,128]{3,2,1,0:T(8,128)S(1)} %get-tuple-element.6.refs_0_, f32[4,32,128]{2,1,0:T(8,128)S(1)} %get-tuple-element.7.refs_1_, f32[16,8,128]{2,1,0:T(8,128)S(1)} %get-tuple-element.8.refs_2_), custom_call_target="tpu_custom_call" | custom-call | tf_op jit(solution)/shard_map/write_out/pallas_call | solution.py:558
